TPU v7x, 128 devices: a whole 4x4x4 slice. The times are simulated.
128 devices in a mesh: gx: 4 (over z), gy: 4 (over x_lo, core), gz: 8 (over y, x_hi).
Axes of the slice: x: 4 (x_hi: 2, x_lo: 2; x = x_hi * 2 + x_lo), y: 4, z: 4, core: 2. Of those that a mesh axis runs over, the one named last changes fastest.
Arguments:
- multipoles: bfloat16 [8, 4, 4, 165, 1024], P('gz', 'gy', 'gx'), may hold values from -6 to 6
- positions: bfloat16 [8, 4, 4, 128, 3, 128], P('gz', 'gy', 'gx'), may hold values from -1 to 1
- masses: bfloat16 [8, 4, 4, 128, 128], P('gz', 'gy', 'gx'), may hold values from -0.5 to 0.5
- m2l_ops: bfloat16 [165, 21120], replicated, may hold values from -0.015625 to 0.015625
- cell_sends: int32 [8, 4, 4, 7, 384], P('gz', 'gy', 'gx'), may hold values from 0 to 1023
- leaf_sends: int32 [8, 4, 4, 7, 16], P('gz', 'gy', 'gx'), may hold values from 0 to 127
- m2l_lists: int32 [8, 4, 4, 1024, 128], P('gz', 'gy', 'gx'), may hold values from 0 to 3711
- near_lists: int32 [8, 4, 4, 128, 8], P('gz', 'gy', 'gx'), may hold values from 0 to 239
- owners: int32 [8, 4, 4, 1024, 1], P('gz', 'gy', 'gx'), may hold values from 0 to 127; in each aligned block of 1024 rows (0 to 1023, 1024 to 2047, ..., all dimensions but the last counted through in order) at most 16 rows name the same one
- owner_boxes: int32 [8, 4, 4, 1024], P('gz', 'gy', 'gx'), may hold values from 0 to 127
Outputs:
- local_exp: float32 [8, 4, 4, 128, 165], P('gz', 'gy', 'gx')
- potential: float32 [8, 4, 4, 128, 128], P('gz', 'gy', 'gx')
Inputs may be any that keep to these rules, and one draw needn't show every extreme that they name: `owners`: among the rows of one device at most 16 name the same owner, and in every draw some owner is named by exactly 16 rows of some device.
All inputs are finite; a program needn't handle non-finite values.
Results may differ from a plain program's by a relative error of at most 0.0003.
Values may be sent and summed in bfloat16 or wider, within the bound.
A program may use at most 128 MiB of HBM per device.

v0:
```python
import math

import jax
import jax.numpy as jnp
import numpy as np
from jax import lax
from jax.sharding import PartitionSpec as P

ORDER = 8


soft_sq = 0.01


def shortened(x):
    return jax.tree.map(lambda a: a.astype(jnp.bfloat16) if a.dtype == jnp.float32 else a, x)


def partner(x, axis, apart):
    return lax.ppermute(x, axis, [(i, i ^ 1 << apart) for i in range(lax.axis_size(axis))])


def side_by_side(arrays, axis, split_dim, concat_dim, along):
    widths = [math.prod(a.shape[along:]) for a in arrays]
    both = jnp.concatenate(
        [a.reshape(*a.shape[:along], w) for a, w in zip(arrays, widths)], axis=along
    )
    filled = lax.all_to_all(both, axis, split_axis=split_dim, concat_axis=concat_dim, tiled=True)
    tiles = jnp.split(filled, [sum(widths[:k]) for k in range(1, len(widths))], axis=along)
    return tuple(
        (b.reshape(*filled.shape[:along], *a.shape[along:]) for a, b in zip(arrays, tiles))
    )


def exponent_table(order):
    entries = []
    for degree_sum in range(order + 1):
        for power_x in range(degree_sum, -1, -1):
            for power_y in range(degree_sum - power_x, -1, -1):
                entries.append((power_x, power_y, degree_sum - power_x - power_y))
    return entries


def shift_table(count):
    entries = []
    for offset in range(count):
        entries.append((offset % 3 - 1, offset // 3 % 3 - 1, offset // 9 - 1))
    return 2.0 * np.array(entries, dtype=np.float32)


def far_field(coords, expansion, order):
    coords_f = coords.astype(jnp.float32)
    powers = [jnp.ones_like(coords_f)]
    for degree in range(order):
        powers.append(powers[-1] * coords_f)
    monomials = jnp.stack(
        [
            powers[ex_a][:, 0] * powers[ex_b][:, 1] * powers[ex_c][:, 2]
            for ex_a, ex_b, ex_c in exponent_table(order)
        ]
    )
    return jnp.einsum("abn,ba->bn", monomials, expansion, precision=lax.Precision.HIGHEST)


def near_group(targets, source_pos, source_mass, shifts):
    target_f = targets.astype(jnp.float32)
    source_f = source_pos.astype(jnp.float32) + shifts[None, :, :, None]
    diff_x = target_f[:, None, 0, :, None] - source_f[:, :, 0, None, :]
    diff_y = target_f[:, None, 1, :, None] - source_f[:, :, 1, None, :]
    diff_z = target_f[:, None, 2, :, None] - source_f[:, :, 2, None, :]
    dist_sq = diff_x * diff_x + diff_y * diff_y + diff_z * diff_z + soft_sq
    weights = source_mass.astype(jnp.float32)[:, :, None, :]
    return jnp.sum(weights * lax.rsqrt(dist_sq), axis=(1, 3))


def near_field(targets, pos_pool, mass_pool, lists, shifts):
    box_count = targets.shape[0]
    group_size = math.gcd(box_count, 16)

    def near_one(packed):
        target_rows, index_rows = packed
        return near_group(target_rows, pos_pool[index_rows], mass_pool[index_rows], shifts)

    result = lax.map(
        near_one,
        (
            targets.reshape(box_count // group_size, group_size, 3, targets.shape[2]),
            lists.reshape(box_count // group_size, group_size, lists.shape[1]),
        ),
    )
    return result.reshape(box_count, targets.shape[2])


def swap_low(outgoing, bit_index):
    return jax.tree.map(
        lambda part, own: part.astype(own.dtype),
        partner(shortened(outgoing), "gx", bit_index),
        outgoing,
    )


def swap_middle(outgoing, bit_index):
    return jax.tree.map(
        lambda part, own: part.astype(own.dtype),
        partner(shortened(outgoing), "gy", bit_index),
        outgoing,
    )


def swap_high(outgoing, bit_index):
    return jax.tree.map(
        lambda part, own: part.astype(own.dtype),
        partner(shortened(outgoing), "gz", bit_index),
        outgoing,
    )


def body(
    multipoles,
    positions,
    masses,
    m2l_ops,
    cell_sends,
    leaf_sends,
    m2l_lists,
    near_lists,
    owners,
    owner_boxes,
):
    cells_rows = jnp.transpose(multipoles[0, 0, 0])
    pos_own = positions[0, 0, 0]
    mass_own = masses[0, 0, 0]
    cell_send = cell_sends[0, 0, 0]
    leaf_send = leaf_sends[0, 0, 0]
    m2l_rows = m2l_lists[0, 0, 0]
    near_rows = near_lists[0, 0, 0]
    owner_rank = owners[0, 0, 0, :, 0]
    owner_box = owner_boxes[0, 0, 0]
    size_x = lax.axis_size("gx")
    size_y = lax.axis_size("gy")
    size_z = lax.axis_size("gz")
    bits_x = size_x.bit_length() - 1
    bits_y = size_y.bit_length() - 1
    bits_z = size_z.bit_length() - 1
    plan = [
        (swap_low, 0, bits_x),
        (swap_middle, bits_x, bits_y),
        (swap_high, bits_x + bits_y, bits_z),
    ]
    received = {}
    for swapper, first_bit, bit_count in plan:
        for bit_index in range(bit_count):
            section = first_bit + bit_index
            outgoing = (
                cells_rows[cell_send[section]],
                pos_own[leaf_send[section]],
                mass_own[leaf_send[section]],
            )
            received[section] = swapper(outgoing, bit_index)
    sections = bits_x + bits_y + bits_z
    cell_pool = jnp.concatenate(
        [cells_rows] + [received[section][0] for section in range(sections)], axis=0
    )
    pos_pool = jnp.concatenate(
        [pos_own] + [received[section][1] for section in range(sections)], axis=0
    )
    mass_pool = jnp.concatenate(
        [mass_own] + [received[section][2] for section in range(sections)], axis=0
    )
    terms_count = cells_rows.shape[1]
    positions_count = m2l_rows.shape[1]
    padded_terms = (terms_count + 127) // 128 * 128
    wide_pool = jnp.pad(cell_pool, ((0, 0), (0, padded_terms - terms_count)))
    ops_wide = jnp.pad(
        m2l_ops.reshape(terms_count, positions_count, terms_count),
        ((0, 0), (0, 0), (0, padded_terms - terms_count)),
    )
    target_rows = m2l_rows.shape[0]
    block_rows = min(128, target_rows)
    block_count = target_rows // block_rows

    def m2l_block(index_rows):
        gathered = wide_pool[index_rows]
        return lax.dot_general(
            gathered, ops_wide, (((1, 2), (1, 2)), ((), ())), preferred_element_type=jnp.float32
        )

    partials = lax.map(m2l_block, m2l_rows.reshape(block_count, block_rows, positions_count))
    partials = partials.reshape(target_rows, terms_count)
    devices = size_x * size_y * size_z
    capacity = 2 * target_rows // devices
    rank_lanes = jnp.arange(devices, dtype=jnp.int32)
    onehot = (owner_rank[:, None] == rank_lanes[None, :]).astype(jnp.float32)
    row_ids = jnp.arange(target_rows, dtype=jnp.int32)
    lower = (row_ids[:, None] > row_ids[None, :]).astype(jnp.float32)
    earlier = jnp.dot(
        lower, onehot, precision=lax.Precision.HIGHEST, preferred_element_type=jnp.float32
    )
    slot_index = jnp.sum(earlier * onehot, axis=1).astype(jnp.int32)
    coord_x = owner_rank % size_x
    coord_y = owner_rank // size_x % size_y
    coord_z = owner_rank // (size_x * size_y)
    joined = (coord_x * size_y + coord_y) * size_z + coord_z
    dest_rows = joined * capacity + slot_index
    slot_ids = jnp.arange(devices * capacity, dtype=jnp.int32)
    placement = (slot_ids[:, None] == dest_rows[None, :]).astype(jnp.float32)
    outgoing_rows = jnp.dot(
        placement, partials, precision=lax.Precision.HIGHEST, preferred_element_type=jnp.float32
    )
    labels = jnp.dot(
        placement,
        owner_box.astype(jnp.float32),
        precision=lax.Precision.HIGHEST,
        preferred_element_type=jnp.float32,
    )
    arrived, arrived_labels = side_by_side(
        (outgoing_rows.reshape(devices, capacity, terms_count), labels.reshape(devices, capacity)),
        ("gx", "gy", "gz"),
        0,
        0,
        2,
    )
    box_count = pos_own.shape[0]
    box_ids = jnp.arange(box_count, dtype=jnp.int32)
    box_hot = (
        box_ids[:, None] == arrived_labels.reshape(devices * capacity).astype(jnp.int32)[None, :]
    ).astype(jnp.float32)
    local_exp = jnp.dot(
        box_hot,
        arrived.reshape(devices * capacity, terms_count),
        precision=lax.Precision.HIGHEST,
        preferred_element_type=jnp.float32,
    )
    shifts = jnp.asarray(shift_table(near_rows.shape[1]), dtype=jnp.float32)
    far = far_field(pos_own, local_exp, ORDER)
    near = near_field(pos_own, pos_pool, mass_pool, near_rows, shifts)
    potential = far - near
    return (local_exp[None, None, None], potential[None, None, None])


def solution(mesh):
    return jax.shard_map(
        body,
        mesh=mesh,
        in_specs=(
            P("gz", "gy", "gx", None, None),
            P("gz", "gy", "gx", None, None, None),
            P("gz", "gy", "gx", None, None),
            P(),
            P("gz", "gy", "gx", None, None),
            P("gz", "gy", "gx", None, None),
            P("gz", "gy", "gx", None, None),
            P("gz", "gy", "gx", None, None),
            P("gz", "gy", "gx", None, None),
            P("gz", "gy", "gx", None),
        ),
        out_specs=(P("gz", "gy", "gx", None, None), P("gz", "gy", "gx", None, None)),
        check_vma=False,
    )
```

profile of v0, /device:TPU:1, one launch (start us, length us, event | category | flops | bytes accessed | tf_op | source)
XLA Modules:
  0.0 1067.9 jit_solution(9170429639888255206)
XLA Ops:
  147.2 31.9 %reshape.3060 = bf16[165,128,165]{2,1,0:T(8,128)(2,1)} reshape(bf16[165,21120]{1,0:T(8,128)(2,1)} %param.18) | data formatting | bytes 13939200 | tf_op jit(solution)/shard_map/reshape | solution.py:175
  179.1 12.7 %copy.167 = bf16[165,128,165]{2,0,1:T(8,128)(2,1)} copy(bf16[165,128,165]{2,1,0:T(8,128)(2,1)} %reshape.3060) | data formatting | bytes 13939200
  192.5 10.3 pad.9.clone
  228.8 7.0 collective-permute-start.16
  264.7 692.9 %while.21 = (s32[]{:T(128)}, f32[8,128,165]{1,0,2:T(8,128)}, s32[8,128,128]{2,1,0:T(8,128)}, bf16[3712,256]{1,0:T(8,128)(2,1)S(1)}, bf16[165,128,256]{2,0,1:T(8,128)(2,1)}, /*index=5*/s32[]{:T(128)}, s32[]{:T(128)}) while((s32[]{:T(128)}, f32[8,128,165]{1,0,2:T(8,128)}, s32[8,128,128]{2,1,0:T(8,128)}, bf16[3712,256]{1,0:T(8,128)(2,1)S(1)}, ...), condition=%wide.region_2.3_spmd, body=%wide.region_1.2_spmd.sunk | while | flops 1384185856 | bytes 36598364 | solution.py:188
  265.5 64.9 %gather_fusion = bf16[16384,256]{1,0:T(8,128)(2,1)} fusion(bf16[3712,256]{1,0:T(8,128)(2,1)S(1)} %get-tuple-element.335, s32[16384]{0:T(1024)S(1)} %fusion.98), kind=kCustom, calls=%fused_computation.clone.1 | custom fusion | bytes 16842752 | tf_op jit(solution)/shard_map/while/body/eval_jaxpr/gather | solution.py:183
  330.4 16.9 %fusion.99 = f32[1,128,165]{1,2,0:T(8,128)S(1)} fusion(bf16[165,128,256]{2,0,1:T(8,128)(2,1)} %get-tuple-element.336, bf16[128,128,256]{2,1,0:T(8,128)(2,1)} %bitcast.825), kind=kOutput, calls=%fused_computation.26.clone.1 | convolution fusion | flops 1384120320 | bytes 19286528 | tf_op jit(solution)/shard_map/while/body/eval_jaxpr/dot_general | solution.py:184
  352.1 64.9 %gather_fusion = bf16[16384,256]{1,0:T(8,128)(2,1)} fusion(bf16[3712,256]{1,0:T(8,128)(2,1)S(1)} %get-tuple-element.335, s32[16384]{0:T(1024)S(1)} %fusion.98), kind=kCustom, calls=%fused_computation.clone.1 | custom fusion | bytes 16842752 | tf_op jit(solution)/shard_map/while/body/eval_jaxpr/gather | solution.py:183
  417.0 16.9 %fusion.99 = f32[1,128,165]{1,2,0:T(8,128)S(1)} fusion(bf16[165,128,256]{2,0,1:T(8,128)(2,1)} %get-tuple-element.336, bf16[128,128,256]{2,1,0:T(8,128)(2,1)} %bitcast.825), kind=kOutput, calls=%fused_computation.26.clone.1 | convolution fusion | flops 1384120320 | bytes 19286528 | tf_op jit(solution)/shard_map/while/body/eval_jaxpr/dot_general | solution.py:184
  438.7 64.9 %gather_fusion = bf16[16384,256]{1,0:T(8,128)(2,1)} fusion(bf16[3712,256]{1,0:T(8,128)(2,1)S(1)} %get-tuple-element.335, s32[16384]{0:T(1024)S(1)} %fusion.98), kind=kCustom, calls=%fused_computation.clone.1 | custom fusion | bytes 16842752 | tf_op jit(solution)/shard_map/while/body/eval_jaxpr/gather | solution.py:183
  503.6 16.9 %fusion.99 = f32[1,128,165]{1,2,0:T(8,128)S(1)} fusion(bf16[165,128,256]{2,0,1:T(8,128)(2,1)} %get-tuple-element.336, bf16[128,128,256]{2,1,0:T(8,128)(2,1)} %bitcast.825), kind=kOutput, calls=%fused_computation.26.clone.1 | convolution fusion | flops 1384120320 | bytes 19286528 | tf_op jit(solution)/shard_map/while/body/eval_jaxpr/dot_general | solution.py:184
  525.2 64.9 %gather_fusion = bf16[16384,256]{1,0:T(8,128)(2,1)} fusion(bf16[3712,256]{1,0:T(8,128)(2,1)S(1)} %get-tuple-element.335, s32[16384]{0:T(1024)S(1)} %fusion.98), kind=kCustom, calls=%fused_computation.clone.1 | custom fusion | bytes 16842752 | tf_op jit(solution)/shard_map/while/body/eval_jaxpr/gather | solution.py:183
  590.1 16.9 %fusion.99 = f32[1,128,165]{1,2,0:T(8,128)S(1)} fusion(bf16[165,128,256]{2,0,1:T(8,128)(2,1)} %get-tuple-element.336, bf16[128,128,256]{2,1,0:T(8,128)(2,1)} %bitcast.825), kind=kOutput, calls=%fused_computation.26.clone.1 | convolution fusion | flops 1384120320 | bytes 19286528 | tf_op jit(solution)/shard_map/while/body/eval_jaxpr/dot_general | solution.py:184
  611.8 64.9 %gather_fusion = bf16[16384,256]{1,0:T(8,128)(2,1)} fusion(bf16[3712,256]{1,0:T(8,128)(2,1)S(1)} %get-tuple-element.335, s32[16384]{0:T(1024)S(1)} %fusion.98), kind=kCustom, calls=%fused_computation.clone.1 | custom fusion | bytes 16842752 | tf_op jit(solution)/shard_map/while/body/eval_jaxpr/gather | solution.py:183
  676.7 16.9 %fusion.99 = f32[1,128,165]{1,2,0:T(8,128)S(1)} fusion(bf16[165,128,256]{2,0,1:T(8,128)(2,1)} %get-tuple-element.336, bf16[128,128,256]{2,1,0:T(8,128)(2,1)} %bitcast.825), kind=kOutput, calls=%fused_computation.26.clone.1 | convolution fusion | flops 1384120320 | bytes 19286528 | tf_op jit(solution)/shard_map/while/body/eval_jaxpr/dot_general | solution.py:184
  698.3 64.9 %gather_fusion = bf16[16384,256]{1,0:T(8,128)(2,1)} fusion(bf16[3712,256]{1,0:T(8,128)(2,1)S(1)} %get-tuple-element.335, s32[16384]{0:T(1024)S(1)} %fusion.98), kind=kCustom, calls=%fused_computation.clone.1 | custom fusion | bytes 16842752 | tf_op jit(solution)/shard_map/while/body/eval_jaxpr/gather | solution.py:183
  763.2 16.9 %fusion.99 = f32[1,128,165]{1,2,0:T(8,128)S(1)} fusion(bf16[165,128,256]{2,0,1:T(8,128)(2,1)} %get-tuple-element.336, bf16[128,128,256]{2,1,0:T(8,128)(2,1)} %bitcast.825), kind=kOutput, calls=%fused_computation.26.clone.1 | convolution fusion | flops 1384120320 | bytes 19286528 | tf_op jit(solution)/shard_map/while/body/eval_jaxpr/dot_general | solution.py:184
  784.9 64.9 %gather_fusion = bf16[16384,256]{1,0:T(8,128)(2,1)} fusion(bf16[3712,256]{1,0:T(8,128)(2,1)S(1)} %get-tuple-element.335, s32[16384]{0:T(1024)S(1)} %fusion.98), kind=kCustom, calls=%fused_computation.clone.1 | custom fusion | bytes 16842752 | tf_op jit(solution)/shard_map/while/body/eval_jaxpr/gather | solution.py:183
  849.8 16.9 %fusion.99 = f32[1,128,165]{1,2,0:T(8,128)S(1)} fusion(bf16[165,128,256]{2,0,1:T(8,128)(2,1)} %get-tuple-element.336, bf16[128,128,256]{2,1,0:T(8,128)(2,1)} %bitcast.825), kind=kOutput, calls=%fused_computation.26.clone.1 | convolution fusion | flops 1384120320 | bytes 19286528 | tf_op jit(solution)/shard_map/while/body/eval_jaxpr/dot_general | solution.py:184
  871.5 64.9 %gather_fusion = bf16[16384,256]{1,0:T(8,128)(2,1)} fusion(bf16[3712,256]{1,0:T(8,128)(2,1)S(1)} %get-tuple-element.335, s32[16384]{0:T(1024)S(1)} %fusion.98), kind=kCustom, calls=%fused_computation.clone.1 | custom fusion | bytes 16842752 | tf_op jit(solution)/shard_map/while/body/eval_jaxpr/gather | solution.py:183
  936.4 16.9 %fusion.99 = f32[1,128,165]{1,2,0:T(8,128)S(1)} fusion(bf16[165,128,256]{2,0,1:T(8,128)(2,1)} %get-tuple-element.336, bf16[128,128,256]{2,1,0:T(8,128)(2,1)} %bitcast.825), kind=kOutput, calls=%fused_computation.26.clone.1 | convolution fusion | flops 1384120320 | bytes 19286528 | tf_op jit(solution)/shard_map/while/body/eval_jaxpr/dot_general | solution.py:184
  965.6 11.2 %all-to-all-start = ((f32[128,16,166]{2,1,0:T(8,128)}), f32[128,16,166]{2,1,0:T(8,128)S(1)}, u32[]{:S(2)}, u32[]{:S(2)}) async-start(f32[128,16,166]{2,1,0:T(8,128)} %copy.139), calls=%async_computation | async-start | bytes 4194304 | tf_op jit(solution)/shard_map/all_to_all | solution.py:28
  976.8 65.9 %while.22 = (s32[]{:T(128)}, f32[8,16,128]{2,1,0:T(8,128)S(1)}, s32[8,16,8]{1,0,2:T(8,128)}, bf16[240,128]{1,0:T(8,128)(2,1)S(1)}, bf16[8,16,3,128]{3,1,0,2:T(8,...) while((s32[]{:T(128)}, f32[8,16,128]{2,1,0:T(8,128)S(1)}, ...), condition=%wide.region_5.6_spmd.clone, body=%wide.region_3.5_spmd.sunk.clone.sunk | while | flops 23188864 | bytes 1455817 | solution.py:84
  980.3 4.8 multiply_reduce_fusion.2
  988.5 4.8 multiply_reduce_fusion.2
  996.7 4.8 multiply_reduce_fusion.2
  1005.0 4.8 multiply_reduce_fusion.2
  1013.2 4.8 multiply_reduce_fusion.2
  1021.4 4.8 multiply_reduce_fusion.2
  1029.7 4.8 multiply_reduce_fusion.2
  1037.9 4.8 multiply_reduce_fusion.2
  1048.0 19.1 %fusion.7 = f32[128,1,128]{2,1,0:T(1,128)S(1)} fusion(f32[128,165,1]{1,2,0:T(1,128)S(1)} %copy.160, f32[165,128,128]{2,1,0:T(8,128)} %constant_dynamic-update-slice_fusion.8), kind=kOutput, calls=%fused_computation.41 | convolution fusion | flops 32440320 | bytes 10963456 | tf_op jit(solution)/shard_map/abn,ba->bn/dot_general | solution.py:62
  (456 shorter events, 280.7 us)
Async XLA Ops:
  0.6 24.4 %copy-start.4 = (bf16[1,1,1,128,128]{4,3,2,1,0:T(8,128)(2,1)S(1)}, bf16[1,1,1,128,128]{4,3,2,1,0:T(8,128)(2,1)}, u32[]{:S(2)}) copy-start(bf16[1,1,1,128,128]{4,3,2,1,0:T(8,128)(2,1)} %param.17) | copy-start | bytes 98308
  0.6 24.5 %copy-start.3 = (bf16[1,1,1,128,3,128]{5,3,4,2,1,0:T(8,128)(2,1)S(1)}, bf16[1,1,1,128,3,128]{5,3,4,2,1,0:T(8,128)(2,1)}, u32[]{:S(2)}) copy-start(bf16[1,1,1,128,3,128]{5,3,4,2,1,0:T(8,128)(2,1)} %param.16) | copy-start | bytes 294916
  0.7 24.5 %copy-start.10 = (s32[1,1,1,1024,1]{3,4,2,1,0:T(1,128)S(1)}, s32[1,1,1,1024,1]{3,4,2,1,0:T(1,128)}, u32[]{:S(2)}) copy-start(s32[1,1,1,1024,1]{3,4,2,1,0:T(1,128)} %param.23) | copy-start | bytes 12292
  4.8 248.2 %collective-permute-start = (bf16[384,165]{1,0:T(8,128)(2,1)S(1)}, bf16[384,165]{1,0:T(8,128)(2,1)S(1)}, u32[]{:S(2)}, u32[]{:S(2)}) collective-permute-start(bf16[384,165]{1,0:T(8,128)(2,1)S(1)} %gather_fusion.3), channel_id=1, source_target_pairs={{0,32},{32,0},{64,96},{96,64},{1,33},{33,1},{65,97},{97,65},{2,34}... | collective-permute-start | bytes 380168 | tf_op jit(solution)/shard_map/ppermute | solution.py:20
  9.4 245.7 %collective-permute-start.1 = (bf16[384,165]{1,0:T(8,128)(2,1)S(1)}, bf16[384,165]{1,0:T(8,128)(2,1)S(1)}, u32[]{:S(2)}, u32[]{:S(2)}) collective-permute-start(bf16[384,165]{1,0:T(8,128)(2,1)S(1)} %gather_fusion.4), channel_id=1, source_target_pairs={{0,64},{32,96},{64,0},{96,32},{1,65},{33,97},{65,1},{97,33},{2,66}... | collective-permute-start | bytes 380168 | tf_op jit(solution)/shard_map/ppermute | solution.py:20
  14.8 243.7 %collective-permute-start.2 = (bf16[384,165]{1,0:T(8,128)(2,1)S(1)}, bf16[384,165]{1,0:T(8,128)(2,1)S(1)}, u32[]{:S(2)}, u32[]{:S(2)}) collective-permute-start(bf16[384,165]{1,0:T(8,128)(2,1)S(1)} %gather_fusion.5), channel_id=1, source_target_pairs={{0,8},{8,0},{16,24},{24,16},{1,9},{9,1},{17,25},{25,17},{2,10},{10... | collective-permute-start | bytes 380168 | tf_op jit(solution)/shard_map/ppermute | solution.py:20
  18.2 241.0 %collective-permute-start.3 = (bf16[384,165]{1,0:T(8,128)(2,1)S(1)}, bf16[384,165]{1,0:T(8,128)(2,1)S(1)}, u32[]{:S(2)}, u32[]{:S(2)}) collective-permute-start(bf16[384,165]{1,0:T(8,128)(2,1)S(1)} %gather_fusion.6), channel_id=1, source_target_pairs={{0,16},{8,24},{16,0},{24,8},{1,17},{9,25},{17,1},{25,9},{2,18},{10... | collective-permute-start | bytes 380168 | tf_op jit(solution)/shard_map/ppermute | solution.py:20
  21.6 181.2 %collective-permute-start.7 = (bf16[16,128]{1,0:T(8,128)(2,1)S(1)}, bf16[16,128]{1,0:T(8,128)(2,1)S(1)}, u32[]{:S(2)}, u32[]{:S(2)}) collective-permute-start(bf16[16,128]{1,0:T(8,128)(2,1)S(1)} %gather_fusion.10), channel_id=1, source_target_pairs={{0,32},{32,0},{64,96},{96,64},{1,33},{33,1},{65,97},{97,65},{2,34}... | collective-permute-start | bytes 12296 | tf_op jit(solution)/shard_map/ppermute | solution.py:20
  21.7 107.3 %copy-start.8 = (s32[128,16]{0,1:T(8,128)}, s32[128,16]{0,1:T(8,128)S(1)}, u32[]{:S(2)}) copy-start(s32[128,16]{0,1:T(8,128)S(1)} %multiply_add_fusion) | copy-start | bytes 24580
  25.8 103.2 %copy-start.12 = (s32[1024]{0:T(1024)}, s32[1024]{0:T(1024)S(1)}, u32[]{:S(2)}) copy-start(s32[1024]{0:T(1024)S(1)} %fusion.53) | copy-start | bytes 12292
  61.6 67.4 %copy-start.14 = (s32[1,1,1,1024]{3,2,1,0:T(1,128)S(1)}, s32[1,1,1,1024]{3,2,1,0:T(1,128)}, u32[]{:S(2)}) copy-start(s32[1,1,1,1024]{3,2,1,0:T(1,128)} %param.24) | copy-start | bytes 12292
  202.8 4.0 collective-permute-start.8
  206.8 2.3 collective-permute-start.9
  209.1 2.5 collective-permute-start.10
  211.5 4.0 collective-permute-start.11
  215.5 2.5 collective-permute-start.12
  218.0 4.0 collective-permute-start.13
  221.9 2.8 collective-permute-start.14
  223.6 38.5 %copy-start = (bf16[240,128]{1,0:T(8,128)(2,1)}, bf16[240,128]{1,0:T(8,128)(2,1)S(1)}, u32[]{:S(2)}) copy-start(bf16[240,128]{1,0:T(8,128)(2,1)S(1)} %constant_dynamic-update-slice_fusion.173) | copy-start | bytes 184324
  224.7 4.0 collective-permute-start.15
  228.8 7.8 collective-permute-start.16
  236.6 2.5 collective-permute-start.17
  239.1 4.0 collective-permute-start.18
  243.2 2.5 collective-permute-start.19
  245.7 4.0 collective-permute-start.20
  249.8 10.1 collective-permute-start.4
  253.0 7.6 collective-permute-start.5
  255.1 7.0 collective-permute-start.6
  264.6 694.2 %copy-start.9 = (s32[128,16]{0,1:T(8,128)S(1)}, s32[128,16]{0,1:T(8,128)}, u32[]{:S(2)}) copy-start(s32[128,16]{0,1:T(8,128)} %copy-done.8) | copy-start | bytes 24580
  264.7 694.2 %copy-start.13 = (s32[1024]{0:T(1024)S(1)}, s32[1024]{0:T(1024)}, u32[]{:S(2)}) copy-start(s32[1024]{0:T(1024)} %copy-done.12) | copy-start | bytes 12292
  264.7 698.8 %copy-start.7 = (f32[128,16,1]{0,2,1:T(1,128)S(1)}, f32[128,16,1]{0,2,1:T(1,128)}, u32[]{:S(2)}) copy-start(f32[128,16,1]{0,2,1:T(1,128)} %fusion.20) | copy-start | bytes 24580
  965.6 77.1 %all-to-all-start = ((f32[128,16,166]{2,1,0:T(8,128)}), f32[128,16,166]{2,1,0:T(8,128)S(1)}, u32[]{:S(2)}, u32[]{:S(2)}) async-start(f32[128,16,166]{2,1,0:T(8,128)} %copy.139), calls=%async_computation | async-start | bytes 4194304 | tf_op jit(solution)/shard_map/all_to_all | solution.py:28
  (5 other events, 89.6 us)
where the time goes:
time: 1080 us; the launch traced here: 1070 us
  local copies, waits for them, and re-layouts  679 us (63%)
  matrix products  165 us (15%)
  other arithmetic  147 us (14%)
  starting transfers between devices  50.8 us (5%)
  waiting for transfers between devices  23.3 us (2%)
    gather x8, local copies, waits for them, and re-layouts, m2l_block(): gathered = wide_pool[index_rows]  519 us
    dot_general x8, matrix products, m2l_block(): lax.dot_general(gathered, ops_wide, (((1, 2), (1, 2)), ((), ())), preferr...  135 us
    unnamed x140, other arithmetic  88 us
    ppermute x21, starting transfers between devices, partner(): lax.ppermute(x, axis, [(i, i ^ 1 << apart) for i in range(lax.axis_size(a...  39.6 us
    reduce_sum x8, other arithmetic, near_group(): return jnp.sum(weights * lax.rsqrt(dist_sq), axis=(1, 3))  38.2 us
    unnamed x79, local copies, waits for them, and re-layouts  35.6 us
    reshape x1, local copies, waits for them, and re-layouts, body(): m2l_ops.reshape(terms_count, positions_count, terms_count)  31.9 us
    dynamic_update_slice x16, local copies, waits for them, and re-layouts, body(): lax.map(m2l_block, m2l_rows.reshape(block_count, block_rows, positions_co...  31.1 us
  transfers between devices with their start and end apart: 22, of which 14 were waited for; matrix products, arithmetic and copies ran while one was open for 24% of the time, Pallas kernels for 0%

commit v1 on v0

v1 whole, which is shorter than its diff:
```python
import functools
import math

import jax
import jax.numpy as jnp
import numpy as np
from jax import lax
from jax.experimental import pallas as pl
from jax.experimental.pallas import tpu as pltpu
from jax.sharding import PartitionSpec as P

ORDER = 8
SOFT_SQ = 0.01
LANES = 128
TAIL = 37
LABEL = 40
BF16, F32, I32 = jnp.bfloat16, jnp.float32, jnp.int32
VMEM_LIMIT = 56 * 2**20


def params(**kw):
    return pltpu.CompilerParams(vmem_limit_bytes=VMEM_LIMIT, **kw)


def vmem():
    return pl.BlockSpec(memory_space=pltpu.VMEM)


def smem():
    return pl.BlockSpec(memory_space=pltpu.SMEM)


def hbm():
    return pl.BlockSpec(memory_space=pl.ANY)


def pick_kernel(sends, psends, sections, cell_idx, leaf_idx, cells, leaves, owner, box, out, slots, pool, stage, leaf_stage):
    count = cells.shape[0]
    for r in range(0, count, 256):
        for j in range(2):
            pool[pl.ds(2 * r + j, 256, stride=2), :] = cells[r : r + 256, j * LANES : (j + 1) * LANES].astype(F32)

    third = sends // 3

    @pl.loop(0, sections)
    def _(b):
        @pl.loop(0, sends // 32)
        def _(g):
            for u in range(32):
                r = g * 32 + u
                c = cell_idx[b * sends + r]
                stage[pl.ds(pl.multiple_of(2 * r, 2), 2), :] = pool[pl.ds(pl.multiple_of(c, 2), 2), :]

        for u in range(psends):
            c = leaf_idx[b * psends + u]
            leaf_stage[4 * u : 4 * u + 4, :] = leaves[pl.ds(pl.multiple_of(c, 4), 4), :]
        out[b, 0:sends, :] = stage[pl.ds(0, sends, stride=2), :].astype(BF16)
        tails = stage[pl.ds(1, third, stride=2), :]
        for g in (1, 2):
            tails += pltpu.roll(stage[pl.ds(2 * g * third + 1, third, stride=2), :], g * TAIL, axis=1)
        out[b, sends : sends + third, :] = tails.astype(BF16)
        out[b, sends + third : sends + third + 4 * psends, :] = leaf_stage[...].astype(BF16)

    rows = owner.shape[0]
    lane = lax.broadcasted_iota(I32, (rows, LANES), 1)
    rank_of_lane = lane // 32 + lane // 8 % 4 * 4 + lane % 8 * 16
    hot = (owner[...] == rank_of_lane).astype(F32)
    hot16 = hot.astype(BF16)
    later = lax.broadcasted_iota(I32, (rows, rows), 0) > lax.broadcasted_iota(I32, (rows, rows), 1)
    earlier = jnp.dot(later.astype(F32).astype(BF16), hot16, preferred_element_type=F32)
    rank = jnp.sum(earlier * hot, axis=1, keepdims=True).astype(I32)
    row = lax.broadcasted_iota(I32, (rows, LANES), 0)
    kind = lane // 16
    value = jnp.where(
        kind == 0, row // 32, jnp.where(kind == 1, row % 32, jnp.where(kind == 2, box[...], jnp.where(kind == 3, 1, 0)))
    )
    value = jnp.where(lane % 16 == rank, value, 0).astype(F32).astype(BF16)
    slots[...] = lax.dot_general(hot16, value, (((0,), (0,)), ((), ())), preferred_element_type=F32)


def pick(cell_idx, leaf_idx, cells, leaves, owner, box, sends, psends, sections):
    width = sends + sends // 3 + 4 * psends
    return pl.pallas_call(
        functools.partial(pick_kernel, sends, psends, sections),
        out_shape=(
            jax.ShapeDtypeStruct((sections, width, LANES), BF16),
            jax.ShapeDtypeStruct((LANES, LANES), F32),
        ),
        in_specs=[smem(), smem(), vmem(), vmem(), vmem(), vmem()],
        out_specs=(vmem(), vmem()),
        scratch_shapes=[
            pltpu.VMEM((2 * cells.shape[0], LANES), F32),
            pltpu.VMEM((2 * sends, LANES), F32),
            pltpu.VMEM((4 * psends, LANES), F32),
        ],
        compiler_params=params(),
        name="pick",
    )(cell_idx, leaf_idx, cells, leaves, owner, box)


def flip(index, bit):
    step = 1 << bit
    return index + step - 2 * step * (index // step % 2)


def exchange_kernel(bits, send, recv, send_sem, recv_sem):
    partners = []
    for name, count in bits:
        for bit in range(count):
            partners.append({name: flip(lax.axis_index(name), bit)})
    barrier = pltpu.get_barrier_semaphore()
    for who in partners:
        pl.semaphore_signal(barrier, inc=1, device_id=who, device_id_type=pl.DeviceIdType.MESH)
    pl.semaphore_wait(barrier, len(partners))
    copies = []
    for b, who in enumerate(partners):
        copy = pltpu.make_async_remote_copy(
            src_ref=send.at[b],
            dst_ref=recv.at[b],
            send_sem=send_sem.at[b],
            recv_sem=recv_sem.at[b],
            device_id=who,
            device_id_type=pl.DeviceIdType.MESH,
        )
        copy.start()
        copies.append(copy)
    for copy in copies:
        copy.wait()


def exchange(send, bits):
    sections = send.shape[0]
    return pl.pallas_call(
        functools.partial(exchange_kernel, bits),
        out_shape=jax.ShapeDtypeStruct(send.shape, send.dtype),
        in_specs=[hbm()],
        out_specs=hbm(),
        scratch_shapes=[pltpu.SemaphoreType.DMA((sections,)), pltpu.SemaphoreType.DMA((sections,))],
        compiler_params=pltpu.CompilerParams(collective_id=0, has_side_effects=True),
        name="exchange",
    )(send)


def panels_kernel(per_step, terms, ops, out):
    g = pl.program_id(0)
    lane = lax.broadcasted_iota(I32, (terms, LANES), 1)
    last = ops.shape[1] - LANES
    for u in range(per_step):
        start = (g * per_step + u) * terms
        base = start // LANES * LANES
        shift = start - base
        back = lax.rem(LANES - shift, LANES)
        tiles = []
        for j in range(3):
            at = pl.multiple_of(jnp.minimum(base + j * LANES, last), LANES)
            tiles.append(pltpu.roll(ops[:, pl.ds(at, LANES)].astype(F32), back, axis=1))
        inside = lane < LANES - shift
        first = jnp.where(inside, tiles[0], tiles[1])
        second = jnp.where(lane < terms - LANES, jnp.where(inside, tiles[1], tiles[2]), 0.0)
        out[0:terms, u * 256 : u * 256 + LANES] = first.astype(BF16)
        out[0:terms, u * 256 + LANES : u * 256 + 256] = second.astype(BF16)
    pad = out.shape[0] - terms
    out[terms:, :] = jnp.zeros((pad, out.shape[1]), BF16)


def panels(ops, positions, rows):
    terms = ops.shape[0]
    per_step = 8
    return pl.pallas_call(
        functools.partial(panels_kernel, per_step, terms),
        grid=(positions // per_step,),
        out_shape=jax.ShapeDtypeStruct((rows, positions * 256), BF16),
        in_specs=[pl.BlockSpec(ops.shape, lambda g: (0, 0), pipeline_mode=pl.Buffered(1))],
        out_specs=pl.BlockSpec((rows, per_step * 256), lambda g: (0, g)),
        compiler_params=params(),
        name="panels",
    )(ops)


def m2l_kernel(
    tb, kc, sends, sections, slots, idx_hbm, fill, cells, recv, ops, ops_before, labels, out, pool, acc, acc_tail, ga, gb, idx_a, idx_b, sem
):
    total = acc.shape[0] - 8
    blocks = total // tb
    chunk = tb * kc
    gs, idxs = (ga, gb), (idx_a, idx_b)
    i, steps = pl.program_id(0), pl.num_programs(0)
    own = cells.shape[0]
    third = sends // 3

    def idx_copy(k, h):
        return pltpu.make_async_copy(idx_hbm.at[k], idxs[h], sem.at[h])

    def gather(g, h, block):
        for r in range(chunk):
            c = idxs[h][block * chunk + r]
            g[2 * r : 2 * r + 2, :] = pool[pl.ds(pl.multiple_of(c, 2), 2), :]

    def multiply(g, block, panel, offset):
        parts = []
        for kk in range(kc):
            for j in range(2):
                parts.append(g[pl.ds(kk * 2 * tb + j, tb, stride=2), :].astype(BF16))
        left = jnp.concatenate(parts, axis=1)
        right = panel[:, offset : offset + kc * 256]
        part = lax.dot_general(left, right, (((1,), (1,)), ((), ())), preferred_element_type=F32)
        at = slice(block * tb, (block + 1) * tb)
        acc[at, :] += part[:, 0:LANES]
        acc_tail[at, 0 : part.shape[1] - LANES] += part[:, LANES:]

    def multiply_queued(q):
        if q < 0:
            multiply(gs[q % 2], q % blocks, ops_before, 0)
        else:
            multiply(gs[q % 2], q % blocks, ops, q // blocks * kc * 256)

    @pl.when(i == 0)
    def _():
        for h in range(2):
            idx_copy(h, h).start()
        acc[...] = jnp.zeros_like(acc)
        acc_tail[...] = jnp.zeros_like(acc_tail)
        gs[1][...] = jnp.zeros_like(gs[1])
        for r in range(0, own, 256):
            for j in range(2):
                pool[pl.ds(2 * r + j, 256, stride=2), :] = cells[r : r + 256, j * LANES : (j + 1) * LANES].astype(F32)

        @pl.loop(0, sections)
        def _(b):
            at = 2 * (own + b * sends)
            pool[pl.ds(pl.multiple_of(at, 2), sends, stride=2), :] = recv[b, 0:sends, :].astype(F32)
            tails = recv[b, sends : sends + third, :].astype(F32)
            lane = lax.broadcasted_iota(I32, tails.shape, 1)
            for g in range(3):
                moved = tails if g == 0 else pltpu.roll(tails, LANES - g * TAIL, axis=1)
                moved = jnp.where(lane < TAIL, moved, 0.0)
                pool[pl.ds(pl.multiple_of(at + 2 * g * third, 2) + 1, third, stride=2), :] = moved

    ahead = jnp.minimum(i + 1, steps - 1)
    for h in range(2):
        idx_copy(2 * i + h, h).wait()
        for block in range(blocks):
            q = h * blocks + block
            multiply_queued(q - 1)
            gather(gs[q % 2], h, block)
        idx_copy(2 * ahead + h, h).start()

    @pl.when(i == steps - 1)
    def _():
        multiply_queued(2 * blocks - 1)
        for h in range(2):
            idx_copy(2 * ahead + h, h).wait()
        low = lax.broadcasted_iota(I32, (1, LANES), 1) < 64

        @pl.loop(0, slots // 16)
        def _(d):
            for s in range(0, 16, 2):
                even = fill[d * 16 + s]
                odd = fill[d * 16 + s + 1]
                out[d, s // 2 : s // 2 + 1, :] = acc[pl.ds(even, 1), :]
                out[d, 8 + s // 2 : 9 + s // 2, :] = acc[pl.ds(odd, 1), :]
                ga[s : s + 1, :] = acc_tail[pl.ds(even, 1), :]
                ga[s + 1 : s + 2, :] = acc_tail[pl.ds(odd, 1), :]
            out[d, 16:24, :] = (
                ga[pl.ds(0, 8, stride=2), :] + pltpu.roll(ga[pl.ds(1, 8, stride=2), :], 64, axis=1) + labels[d]
            )


def m2l(idx, fill, cells, recv, ops, labels, tb, kc, sends):
    rows, width = ops.shape
    positions = width // 256
    total = idx.shape[0] * idx.shape[1] // positions
    sections = recv.shape[0]
    slots = fill.shape[0]
    cells_all = cells.shape[0] + sections * sends
    steps = positions // kc // 2
    return pl.pallas_call(
        functools.partial(m2l_kernel, tb, kc, sends, sections, slots),
        grid=(steps,),
        out_shape=jax.ShapeDtypeStruct((slots // 16, 24, LANES), F32),
        in_specs=[
            hbm(),
            smem(),
            pl.BlockSpec(cells.shape, lambda i: (0, 0), pipeline_mode=pl.Buffered(1)),
            pl.BlockSpec(recv.shape, lambda i: (0, 0, 0), pipeline_mode=pl.Buffered(1)),
            pl.BlockSpec((rows, 2 * kc * 256), lambda i: (0, i)),
            pl.BlockSpec((rows, kc * 256), lambda i: (0, jnp.maximum(2 * i - 1, 0))),
            pl.BlockSpec(labels.shape, lambda i: (0, 0, 0), pipeline_mode=pl.Buffered(1)),
        ],
        out_specs=pl.BlockSpec((slots // 16, 24, LANES), lambda i: (0, 0, 0)),
        scratch_shapes=[
            pltpu.VMEM((2 * cells_all, LANES), F32),
            pltpu.VMEM((total + 8, LANES), F32),
            pltpu.VMEM((total + 8, LANES), F32),
            pltpu.VMEM((2 * tb * kc, LANES), F32),
            pltpu.VMEM((2 * tb * kc, LANES), F32),
            pltpu.SMEM((total * kc,), I32),
            pltpu.SMEM((total * kc,), I32),
            pltpu.SemaphoreType.DMA((2,)),
        ],
        compiler_params=params(),
        name="m2l",
    )(idx, fill, cells, recv, ops, ops, labels)


def shift_of(k):
    return 2.0 * (k % 3 - 1), 2.0 * (k // 3 % 3 - 1), 2.0 * (k // 9 - 1)


def near_kernel(per_step, lists, targets, leaves, out):
    neighbours = 8
    step = pl.program_id(0)
    half = LANES // 2
    for u in range(per_step):
        cols = []
        for c in range(3):
            cols.append(jnp.transpose(jnp.broadcast_to(targets[u, c : c + 1, :], (LANES, LANES))))
        for part in range(2):
            mine = [col[part * half : (part + 1) * half] for col in cols]
            total = jnp.zeros((half, LANES), F32)
            for k in range(neighbours):
                at = lists[(step * per_step + u) * neighbours + k]
                dist = None
                for c, s in enumerate(shift_of(k)):
                    source = leaves[pl.ds(at + c, 1), :] + s
                    diff = mine[c] - source
                    dist = diff * diff if dist is None else dist + diff * diff
                total += leaves[pl.ds(at + 3, 1), :] * lax.rsqrt(dist + SOFT_SQ)
            out[u : u + 1, part * half : (part + 1) * half] = jnp.sum(jnp.transpose(total), axis=0, keepdims=True)


def near_field(lists, targets, leaves):
    boxes = targets.shape[0]
    per_step = 8
    return pl.pallas_call(
        functools.partial(near_kernel, per_step),
        grid=(boxes // per_step,),
        out_shape=jax.ShapeDtypeStruct((boxes, LANES), F32),
        in_specs=[
            smem(),
            pl.BlockSpec((per_step, 4, LANES), lambda i: (i, 0, 0)),
            pl.BlockSpec(leaves.shape, lambda i: (0, 0), pipeline_mode=pl.Buffered(1)),
        ],
        out_specs=pl.BlockSpec((per_step, LANES), lambda i: (i, 0)),
        compiler_params=params(),
        cost_estimate=pl.CostEstimate(flops=2**28, bytes_accessed=2**20, transcendentals=2**24),
        name="near",
    )(lists, targets, leaves)


def term_index(order):
    table = {}
    for degree in range(order + 1):
        for i in range(degree, -1, -1):
            for j in range(degree - i, -1, -1):
                table[(i, j, degree - i - j)] = len(table)
    return table


def pieces(x):
    high = x.astype(BF16)
    rest = x - high.astype(F32)
    middle = rest.astype(BF16)
    return high, middle, (rest - middle.astype(F32)).astype(BF16)


def final_kernel(order, arrived, coords, near, local, potential):
    sources = arrived.shape[0]
    rows = sources * 8
    tails = arrived[:, 16:24, :].reshape(rows, LANES)
    lane = lax.broadcasted_iota(I32, (rows, LANES), 1).astype(F32)
    sums = []
    for half in range(2):
        label = tails[:, 64 * half + LABEL : 64 * half + LABEL + 1]
        hot = jnp.where(lane == label, 1.0, 0.0).astype(BF16)
        body = arrived[:, 8 * half : 8 * half + 8, :].reshape(rows, LANES)
        both = jnp.concatenate([body, tails], axis=1)
        got = None
        for piece in pieces(both):
            part = lax.dot_general(hot, piece, (((0,), (0,)), ((), ())), preferred_element_type=F32)
            got = part if got is None else got + part
        sums.append(got)
    first = sums[0][:, 0:LANES] + sums[1][:, 0:LANES]
    rest = sums[0][:, LANES:256] + pltpu.roll(sums[1][:, LANES:256], 64, axis=1)
    local[:, 0:LANES] = first
    local[:, LANES : LANES + TAIL] = rest[:, 0:TAIL]
    terms = term_index(order)

    @pl.loop(0, local.shape[0] // 8)
    def _(g):
        box = pl.ds(pl.multiple_of(g * 8, 8), 8)
        head = local[box, 0:LANES]
        tail = local[box, LANES : LANES + TAIL]
        x, y, z = (coords[c, box, :] for c in range(3))

        def coefficient(i, j, m):
            a = terms[(i, j, m)]
            column = head[:, a : a + 1] if a < LANES else tail[:, a - LANES : a - LANES + 1]
            return jnp.broadcast_to(column, (8, LANES))

        in_z = None
        for m in range(order, -1, -1):
            in_y = None
            for j in range(order - m, -1, -1):
                in_x = None
                for i in range(order - m - j, -1, -1):
                    c = coefficient(i, j, m)
                    in_x = c if in_x is None else in_x * x + c
                in_y = in_x if in_y is None else in_y * y + in_x
            in_z = in_y if in_z is None else in_z * z + in_y
        potential[box, :] = in_z - near[box, :]


def finish(arrived, coords, near, terms):
    boxes = near.shape[0]
    return pl.pallas_call(
        functools.partial(final_kernel, ORDER),
        out_shape=(jax.ShapeDtypeStruct((boxes, terms), F32), jax.ShapeDtypeStruct((boxes, LANES), F32)),
        in_specs=[vmem(), vmem(), vmem()],
        out_specs=(vmem(), vmem()),
        compiler_params=params(),
        name="finish",
    )(arrived, coords, near)


def body(
    multipoles, positions, masses, m2l_ops, cell_sends, leaf_sends, m2l_lists, near_lists, owners, owner_boxes
):
    terms, own = multipoles.shape[3:]
    sections, sends = cell_sends.shape[3:]
    psends = leaf_sends.shape[4]
    total, positions_count = m2l_lists.shape[3:]
    boxes = positions.shape[3]
    bits = tuple((name, lax.axis_size(name).bit_length() - 1) for name in ("gx", "gy", "gz"))
    devices = 1 << sum(count for _, count in bits)

    cells = jnp.pad(jnp.transpose(multipoles[0, 0, 0]), ((0, 0), (0, 256 - terms)))
    leaf_own = jnp.concatenate([positions[0, 0, 0], masses[0, 0, 0][:, None, :]], axis=1).astype(F32)
    send, slots = pick(
        cell_sends[0, 0, 0].reshape(-1) * 2,
        leaf_sends[0, 0, 0].reshape(-1) * 4,
        cells,
        leaf_own.reshape(boxes * 4, LANES),
        owners[0, 0, 0],
        owner_boxes[0, 0, 0][:, None],
        sends,
        psends,
        sections,
    )
    recv = exchange(send, bits)
    tb, kc = 512, 2
    idx = jnp.transpose(m2l_lists[0, 0, 0]).reshape(positions_count // kc, kc, total // tb, tb)
    idx = 2 * jnp.transpose(idx, (0, 2, 1, 3)).reshape(positions_count // kc, kc * total)
    used = slots[:, 48:64] > 0.5
    fill = jnp.where(used, slots[:, 0:16] * 32.0 + slots[:, 16:32], float(total)).astype(I32).reshape(-1)
    label = jnp.where(used, slots[:, 32:48], -1.0).reshape(devices, 8, 2, 1)
    at_label = jnp.arange(64, dtype=I32) == LABEL
    labels = jnp.where(at_label, label, 0.0).reshape(devices, 8, LANES)
    wide_ops = panels(m2l_ops, positions_count, 168)
    payload = m2l(idx, fill, cells, recv, wide_ops, labels, tb, kc, sends)
    arrived = lax.all_to_all(payload, ("gx", "gy", "gz"), split_axis=0, concat_axis=0, tiled=True)
    got = recv[:, sends + sends // 3 :, :].astype(F32).reshape(sections * psends * 4, LANES)
    leaves = jnp.concatenate([leaf_own.reshape(boxes * 4, LANES), got], axis=0)
    near = near_field(near_lists[0, 0, 0].reshape(-1) * 4, leaf_own, leaves)
    coords = jnp.transpose(leaf_own[:, 0:3], (1, 0, 2))
    local, potential = finish(arrived, coords, near, terms)
    return local[None, None, None], potential[None, None, None]


def solution(mesh):
    five = P("gz", "gy", "gx", None, None)
    six = P("gz", "gy", "gx", None, None, None)
    return jax.shard_map(
        body,
        mesh=mesh,
        in_specs=(five, six, five, P(), five, five, five, five, five, P("gz", "gy", "gx", None)),
        out_specs=(five, five),
        check_vma=False,
    )
```

time: 1080 us -> 231 us (0.21); the launches traced: 1070 us -> 230 us
  local copies, waits for them, and re-layouts: 679 us -> 13.8 us
  Pallas kernels: 0 us -> 200 us
  matrix products: 165 us -> 0 us
  other arithmetic: 147 us -> 7.18 us
  starting transfers between devices: 50.8 us -> 7.99 us
  waiting for transfers between devices: 23.3 us -> 0.01 us
    gather x52 -> x0, local copies, waits for them, and re-layouts: 554 us -> none  [the longest x8 519 us: m2l_block(): gathered = wide_pool[index_rows]]
    pallas_call x0 -> x6, Pallas kernels: none -> 200 us  [the longest x1 116 us: m2l(): pl.pallas_call(functools.partial(m2l_kernel, tb, kc, sends, sections, slo...]
    dot_general x13 -> x0, matrix products: 165 us -> none  [the longest x8 135 us: m2l_block(): lax.dot_general(gathered, ops_wide, (((1, 2), (1, 2)), ((), ())), preferr...]
    unnamed x140 -> x0, other arithmetic: 88 us -> none
    ppermute x21 -> x0, starting transfers between devices: 39.6 us -> none  [partner(): lax.ppermute(x, axis, [(i, i ^ 1 << apart) for i in range(lax.axis_size(a...]
    reduce_sum x8 -> x0, other arithmetic: 38.2 us -> none  [near_group(): return jnp.sum(weights * lax.rsqrt(dist_sq), axis=(1, 3))]
    reshape x2 -> x1, local copies, waits for them, and re-layouts: 33.1 us -> 0.68 us  [body(): jnp.where(used, slots[:, 0:16] * 32.0 + slots[:, 16:32], float(total))]
    unnamed x79 -> x12, local copies, waits for them, and re-layouts: 35.6 us -> 3.99 us
  transfers between devices with their start and end apart: 22 -> 1, of which waited for: 14 -> 0; matrix products, arithmetic and copies ran while one was open for 24% -> 1% of each run, Pallas kernels for 0% -> 18%
where the time goes in v1:
time: 231 us; the launch traced here: 230 us
  Pallas kernels  200 us (87%)
  local copies, waits for them, and re-layouts  13.8 us (6%)
  starting transfers between devices  7.99 us (3%)
  other arithmetic  7.18 us (3%)
    pallas_call x1, Pallas kernels, m2l(): pl.pallas_call(functools.partial(m2l_kernel, tb, kc, sends, sections, slo...  116 us
    pallas_call x1, Pallas kernels, near_field(): pl.pallas_call(functools.partial(near_kernel, per_step), grid=(boxes // p...  40.5 us
    pallas_call x1, Pallas kernels, exchange(): pl.pallas_call(functools.partial(exchange_kernel, bits), out_shape=jax.Sh...  14.2 us
    pallas_call x1, Pallas kernels, panels(): pl.pallas_call(functools.partial(panels_kernel, per_step, terms), grid=(p...  13.6 us
    pallas_call x1, Pallas kernels, finish(): pl.pallas_call(functools.partial(final_kernel, ORDER), out_shape=(jax.Sha...  9.12 us
    all_to_all x1, starting transfers between devices, body(): lax.all_to_all(payload, ('gx', 'gy', 'gz'), split_axis=0, concat_axis=0,...  7.99 us
    pallas_call x1, Pallas kernels, pick(): pl.pallas_call(functools.partial(pick_kernel, sends, psends, sections), o...  7.28 us
  transfers between devices with their start and end apart: 1, of which 0 were waited for; matrix products, arithmetic and copies ran while one was open for 1% of the time, Pallas kernels for 18%

profile of v1, /device:TPU:1, one launch (start us, length us, event | category | flops | bytes accessed | tf_op | source)
XLA Modules:
  0.0 230.2 jit_solution(17840412139308082787)
XLA Ops:
  0.8 0.7 multiply_reduce_fusion.1
  1.5 0.7 mul.55.leaf_idx
  2.1 0.7 multiply_reduce_fusion
  2.9 0.6 mul.52.cell_idx
  3.5 0.9 maximum_convert_fusion
  4.4 0.9 copy.19.targets
  5.3 1.2 copy.18
  6.5 1.1 multiply_bitcast_fusion
  7.5 0.2 copy.16
  7.8 0.4 mul.47
  8.2 0.3 copy.17
  8.5 1.2 mul.49.idx_hbm
  9.7 1.0 copy.20.owner
  10.8 1.0 copy.21.box
  11.8 0.9 pad.4.cells
  12.6 7.3 %pick.1 = (bf16[7,576,128]{2,1,0:T(8,128)(2,1)}, f32[128,128]{1,0:T(8,128)}) custom-call(s32[2688]{0:T(1024)} %mul.52.cell_idx, s32[112]{0:T(128)} %mul.55.leaf_idx, bf16[1024,256]{1,0:T(8,128)(2,1)} %pad.4.cells, f32[512,128]{1,0:T(8,128)} %bitcast.24, s32[1024,1]{1,0:T(8,128)} %copy.20.owner, s32[1024,1]{1,0:T(8,128)} %copy.21.box), custom_call_target="tpu_custom_call" | custom-call | tf_op jit(solution)/shard_map/pick/pallas_call | solution.py:83
  19.9 14.2 %exchange.1.recv = bf16[7,576,128]{2,1,0:T(8,128)(2,1)} custom-call(bf16[7,576,128]{2,1,0:T(8,128)(2,1)} %get-tuple-element.7.send), custom_call_target="tpu_custom_call" | custom-call | tf_op jit(solution)/shard_map/exchange/pallas_call | solution.py:133
  34.2 1.0 slice_select_fusion
  35.2 1.0 select_convert_fusion
  36.3 0.7 reshape.35.fill
  37.0 0.2 copy.23
  37.2 13.6 %panels.1.ops.ops_before = bf16[168,32768]{1,0:T(8,128)(2,1)} custom-call(bf16[165,21120]{1,0:T(8,128)(2,1)} %ops.1), custom_call_target="tpu_custom_call" | custom-call | tf_op jit(solution)/shard_map/panels/pallas_call | solution.py:169
  50.8 0.8 broadcast_select_fusion.labels
  51.6 115.7 %m2l.1 = f32[128,24,128]{2,1,0:T(8,128)} custom-call(s32[64,2048]{1,0:T(8,128)} %mul.49.idx_hbm, s32[2048]{0:T(1024)} %reshape.35.fill, bf16[1024,256]{1,0:T(8,128)(2,1)} %pad.4.cells, bf16[7,576,128]{2,1,0:T(8,128)(2,1)} %exchange.1.recv, bf16[168,32768]{1,0:T(8,128)(2,1)} %panels.1.ops.ops_before, bf16[168,32768]{1,0:T(8,128)(2,1)} %panels.1.ops.ops_before, ...), custom_call_target="tpu_custom_call" | custom-call | tf_op jit(solution)/shard_map/m2l/pallas_call | solution.py:277
  167.4 8.0 %all-to-all-start = ((f32[128,24,128]{2,1,0:T(8,128)}), f32[128,24,128]{2,1,0:T(8,128)S(1)}, u32[]{:S(2)}, u32[]{:S(2)}) async-start(f32[128,24,128]{2,1,0:T(8,128)} %m2l.1), calls=%async_computation | async-start | bytes 3145728 | tf_op jit(solution)/shard_map/all_to_all | solution.py:461
  175.5 0.7 mul.60.lists
  176.2 0.8 pad_maximum_fusion.leaves
  177.0 40.5 %near.1 = f32[128,128]{1,0:T(8,128)} custom-call(s32[1024]{0:T(1024)} %mul.60.lists, f32[128,4,128]{2,1,0:T(4,128)} %copy.19.targets, f32[960,128]{1,0:T(8,128)} %pad_maximum_fusion.leaves), custom_call_target="tpu_custom_call" | custom-call | flops 268435456 | bytes 1048576 | tf_op jit(solution)/shard_map/near/pallas_call | solution.py:335
  217.6 0.7 slice_bitcast_fusion.coords
  218.3 1.2 copy-done
  219.4 9.1 %finish.1 = (f32[128,165]{1,0:T(8,128)}, f32[128,128]{1,0:T(8,128)}) custom-call(f32[128,24,128]{2,1,0:T(8,128)} %copy-done, f32[3,128,128]{2,1,0:T(8,128)} %slice_bitcast_fusion.coords, f32[128,128]{1,0:T(8,128)} %near.1), custom_call_target="tpu_custom_call" | custom-call | tf_op jit(solution)/shard_map/finish/pallas_call | solution.py:416
  228.6 1.6 copy.26
  (20 shorter events, 0.3 us)
Async XLA Ops:
  0.6 9.1 %copy-start.2 = (s32[1,1,1,1024,1]{3,4,2,1,0:T(1,128)S(1)}, s32[1,1,1,1024,1]{3,4,2,1,0:T(1,128)}, u32[]{:S(2)}) copy-start(s32[1,1,1,1024,1]{3,4,2,1,0:T(1,128)} %param.18) | copy-start | bytes 12292
  0.6 10.1 %copy-start.3 = (s32[1,1,1,1024]{3,2,1,0:T(1,128)S(1)}, s32[1,1,1,1024]{3,2,1,0:T(1,128)}, u32[]{:S(2)}) copy-start(s32[1,1,1,1024]{3,2,1,0:T(1,128)} %param.19) | copy-start | bytes 12292
  51.6 123.7 %copy-start.4 = (s32[1,1,1,128,8]{3,4,2,1,0:T(8,128)S(1)}, s32[1,1,1,128,8]{3,4,2,1,0:T(8,128)}, u32[]{:S(2)}) copy-start(s32[1,1,1,128,8]{3,4,2,1,0:T(8,128)} %param.17) | copy-start | bytes 12292
  51.6 124.5 %slice-start = ((bf16[7,576,128]{2,1,0:T(8,128)(2,1)}), bf16[7,64,128]{2,1,0:T(8,128)(2,1)S(1)}, s32[]{:S(2)}) async-start(bf16[7,576,128]{2,1,0:T(8,128)(2,1)} %exchange.1.recv), calls=%async_computation.1 | async-start | bytes 229376 | tf_op jit(solution)/shard_map/slice | solution.py:462
  51.6 124.6 %copy-start.1 = (f32[128,4,128]{2,1,0:T(4,128)S(1)}, f32[128,4,128]{2,1,0:T(4,128)}, u32[]{:S(2)}) copy-start(f32[128,4,128]{2,1,0:T(4,128)} %copy.19.targets) | copy-start | bytes 786436
  167.4 50.9 %all-to-all-start = ((f32[128,24,128]{2,1,0:T(8,128)}), f32[128,24,128]{2,1,0:T(8,128)S(1)}, u32[]{:S(2)}, u32[]{:S(2)}) async-start(f32[128,24,128]{2,1,0:T(8,128)} %m2l.1), calls=%async_computation | async-start | bytes 3145728 | tf_op jit(solution)/shard_map/all_to_all | solution.py:461
  218.3 1.2 copy-start

commit v2 on v1

v2 whole, which is shorter than its diff:
```python
import functools

import jax
import jax.numpy as jnp
import numpy as np
from jax import lax
from jax.experimental import pallas as pl
from jax.experimental.pallas import tpu as pltpu
from jax.sharding import PartitionSpec as P

ORDER = 8
SOFT_SQ = 0.01
LANES = 128
TAIL = 37
LABEL = 40
BF16, F32, I32 = jnp.bfloat16, jnp.float32, jnp.int32
VMEM_LIMIT = 56 * 2**20


def params(**kw):
    return pltpu.CompilerParams(vmem_limit_bytes=VMEM_LIMIT, **kw)


def vmem():
    return pl.BlockSpec(memory_space=pltpu.VMEM)


def smem():
    return pl.BlockSpec(memory_space=pltpu.SMEM)


def hbm():
    return pl.BlockSpec(memory_space=pl.ANY)


def pick_kernel(sends, psends, sections, cell_idx, leaf_idx, terms, leaves, owner, box, out, pool, fill, labels, stage, leaf_stage):
    count = terms.shape[1]
    for r in range(0, count, 256):
        first = jnp.transpose(terms[0:LANES, r : r + 256].astype(F32))
        rest = terms[LANES:, r : r + 256].astype(F32)
        pad = jnp.zeros((LANES - rest.shape[0], 256), F32)
        pool[pl.ds(2 * r, 256, stride=2), :] = first
        pool[pl.ds(2 * r + 1, 256, stride=2), :] = jnp.transpose(jnp.concatenate([rest, pad], axis=0))

    third = sends // 3

    @pl.loop(0, sections)
    def _(b):
        @pl.loop(0, sends // 32)
        def _(g):
            for u in range(32):
                r = g * 32 + u
                c = cell_idx[b, r] * 2
                stage[pl.ds(pl.multiple_of(2 * r, 2), 2), :] = pool[pl.ds(pl.multiple_of(c, 2), 2), :]

        for u in range(psends):
            c = leaf_idx[b, u] * 4
            leaf_stage[4 * u : 4 * u + 4, :] = leaves[pl.ds(pl.multiple_of(c, 4), 4), :]
        out[b, 0:sends, :] = stage[pl.ds(0, sends, stride=2), :].astype(BF16)
        tails = stage[pl.ds(1, third, stride=2), :]
        for g in (1, 2):
            tails += pltpu.roll(stage[pl.ds(2 * g * third + 1, third, stride=2), :], g * TAIL, axis=1)
        out[b, sends : sends + third, :] = tails.astype(BF16)
        out[b, sends + third : sends + third + 4 * psends, :] = leaf_stage[...].astype(BF16)

    rows = owner.shape[1]
    line = lax.broadcasted_iota(I32, (LANES, rows), 0)
    rank_of_line = line // 32 + line // 8 % 4 * 4 + line % 8 * 16
    hot = jnp.where(owner[...] == rank_of_line, 1.0, 0.0)
    hot16 = hot.astype(BF16)
    sooner = lax.broadcasted_iota(I32, (rows, rows), 0) < lax.broadcasted_iota(I32, (rows, rows), 1)
    earlier = jnp.dot(hot16, jnp.where(sooner, 1.0, 0.0).astype(BF16), preferred_element_type=F32)
    rank = jnp.sum(earlier * hot, axis=0, keepdims=True).astype(I32)
    row = lax.broadcasted_iota(I32, (LANES, rows), 1)
    kind = line // 16
    value = jnp.where(
        kind == 0, row // 32, jnp.where(kind == 1, row % 32, jnp.where(kind == 2, box[...], jnp.where(kind == 3, 1, 0)))
    )
    value = jnp.where(line % 16 == rank, value, 0).astype(F32).astype(BF16)
    slots = lax.dot_general(hot16, value, (((1,), (1,)), ((), ())), preferred_element_type=F32)
    used = pltpu.roll(slots, LANES - 48, axis=1) > 0.5
    at = slots * 32.0 + pltpu.roll(slots, LANES - 16, axis=1)
    fill[...] = jnp.where(used, at, float(rows)).astype(I32)
    label = jnp.where(used, pltpu.roll(slots, LANES - 32, axis=1), -1.0)
    lane = lax.broadcasted_iota(I32, (LANES, LANES), 1)
    for j in range(8):
        labels[j * LANES : (j + 1) * LANES, :] = jnp.where(
            lane == LABEL,
            label[:, 2 * j : 2 * j + 1],
            jnp.where(lane == 64 + LABEL, label[:, 2 * j + 1 : 2 * j + 2], 0.0),
        )


def pick(cell_idx, leaf_idx, terms, leaves, owner, box):
    sections, sends = cell_idx.shape
    psends = leaf_idx.shape[1]
    width = sends + sends // 3 + 4 * psends
    return pl.pallas_call(
        functools.partial(pick_kernel, sends, psends, sections),
        out_shape=(
            jax.ShapeDtypeStruct((sections, width, LANES), BF16),
            jax.ShapeDtypeStruct((2 * terms.shape[1], LANES), F32),
            jax.ShapeDtypeStruct((LANES, LANES), I32),
            jax.ShapeDtypeStruct((8 * LANES, LANES), F32),
        ),
        in_specs=[smem(), smem(), vmem(), vmem(), vmem(), vmem()],
        out_specs=(vmem(),) * 4,
        scratch_shapes=[
            pltpu.VMEM((2 * sends, LANES), F32),
            pltpu.VMEM((4 * psends, LANES), F32),
        ],
        compiler_params=params(),
        name="pick",
    )(cell_idx, leaf_idx, terms, leaves, owner, box)


def flip(index, bit):
    step = 1 << bit
    return index + step - 2 * step * (index // step % 2)


def exchange_kernel(bits, send, recv, send_sem, recv_sem):
    partners = []
    for name, count in bits:
        for bit in range(count):
            partners.append({name: flip(lax.axis_index(name), bit)})
    barrier = pltpu.get_barrier_semaphore()
    for who in partners:
        pl.semaphore_signal(barrier, inc=1, device_id=who, device_id_type=pl.DeviceIdType.MESH)
    pl.semaphore_wait(barrier, len(partners))
    copies = []
    for b, who in enumerate(partners):
        copy = pltpu.make_async_remote_copy(
            src_ref=send.at[b],
            dst_ref=recv.at[b],
            send_sem=send_sem.at[b],
            recv_sem=recv_sem.at[b],
            device_id=who,
            device_id_type=pl.DeviceIdType.MESH,
        )
        copy.start()
        copies.append(copy)
    for copy in copies:
        copy.wait()


def exchange(send, bits):
    sections = send.shape[0]
    return pl.pallas_call(
        functools.partial(exchange_kernel, bits),
        out_shape=jax.ShapeDtypeStruct(send.shape, send.dtype),
        in_specs=[hbm()],
        out_specs=hbm(),
        scratch_shapes=[pltpu.SemaphoreType.DMA((sections,)), pltpu.SemaphoreType.DMA((sections,))],
        compiler_params=pltpu.CompilerParams(collective_id=0, has_side_effects=True),
        name="exchange",
    )(send)


def m2l_kernel(
    tb, kc, sends, terms, idx_hbm, fill, own_hbm, recv, ops_hbm, labels, out,
    pool, acc, acc_tail, ga, gb, idx_a, idx_b, window_a, window_b, panel_a, panel_b, sem, own_sem, window_sem,
):
    total = acc.shape[0] - 8
    blocks = total // tb
    chunk = tb * kc
    gs, idxs = (ga, gb), (idx_a, idx_b)
    windows, panels = (window_a, window_b), (panel_a, panel_b)
    i, steps = pl.program_id(0), pl.num_programs(0)
    own = own_hbm.shape[0] // 2
    third = sends // 3
    width = window_a.shape[1]
    last = ops_hbm.shape[1] - width

    def idx_copy(k, h):
        return pltpu.make_async_copy(idx_hbm.at[k], idxs[h], sem.at[h])

    def window_at(n):
        return jnp.minimum(n * (kc * terms) // LANES * LANES, last)

    def window_copy(n, h):
        at = pl.multiple_of(window_at(n), LANES)
        return pltpu.make_async_copy(ops_hbm.at[:, pl.ds(at, width)], windows[h], window_sem.at[h])

    def build(n, h):
        lane = lax.broadcasted_iota(I32, (terms, LANES), 1)
        for u in range(kc):
            start = (n * kc + u) * terms - window_at(n)
            base = start // LANES
            shift = start - base * LANES
            back = lax.rem(LANES - shift, LANES)
            tiles = []
            for j in range(3):
                at = pl.multiple_of(jnp.minimum(base + j, width // LANES - 1) * LANES, LANES)
                tiles.append(pltpu.roll(windows[h][:, pl.ds(at, LANES)].astype(F32), back, axis=1))
            inside = lane < LANES - shift
            first = jnp.where(inside, tiles[0], tiles[1])
            second = jnp.where(lane < terms - LANES, jnp.where(inside, tiles[1], tiles[2]), 0.0)
            panels[h][0:terms, u * 256 : u * 256 + LANES] = first.astype(BF16)
            panels[h][0:terms, u * 256 + LANES : u * 256 + 256] = second.astype(BF16)

    def gather(g, h, block):
        for r in range(chunk):
            c = idxs[h][block * chunk + r]
            g[2 * r : 2 * r + 2, :] = pool[pl.ds(pl.multiple_of(c, 2), 2), :]

    def multiply(g, block, panel):
        parts = []
        for kk in range(kc):
            for j in range(2):
                parts.append(g[pl.ds(kk * 2 * tb + j, tb, stride=2), :].astype(BF16))
        left = jnp.concatenate(parts, axis=1)
        part = lax.dot_general(left, panel[...], (((1,), (1,)), ((), ())), preferred_element_type=F32)
        at = slice(block * tb, (block + 1) * tb)
        acc[at, :] += part[:, 0:LANES]
        acc_tail[at, 0 : part.shape[1] - LANES] += part[:, LANES:]

    def multiply_queued(q):
        multiply(gs[q % 2], q % blocks, panels[q // blocks % 2])

    ahead = jnp.minimum(i + 1, steps - 1)

    @pl.when(i == 0)
    def _():
        own_copy = pltpu.make_async_copy(own_hbm, pool.at[0 : 2 * own], own_sem)
        own_copy.start()
        for h in range(2):
            idx_copy(h, h).start()
            window_copy(h, h).start()
        acc[...] = jnp.zeros_like(acc)
        acc_tail[...] = jnp.zeros_like(acc_tail)
        gs[1][...] = jnp.zeros_like(gs[1])
        for panel in panels:
            panel[...] = jnp.zeros_like(panel)

        @pl.loop(0, recv.shape[0])
        def _(b):
            at = 2 * (own + b * sends)
            pool[pl.ds(pl.multiple_of(at, 2), sends, stride=2), :] = recv[b, 0:sends, :].astype(F32)
            tails = recv[b, sends : sends + third, :].astype(F32)
            lane = lax.broadcasted_iota(I32, tails.shape, 1)
            for g in range(3):
                moved = tails if g == 0 else pltpu.roll(tails, LANES - g * TAIL, axis=1)
                moved = jnp.where(lane < TAIL, moved, 0.0)
                pool[pl.ds(pl.multiple_of(at + 2 * g * third, 2) + 1, third, stride=2), :] = moved

        own_copy.wait()

    for h in range(2):
        idx_copy(2 * i + h, h).wait()
        window_copy(2 * i + h, h).wait()
        build(2 * i + h, h)
        for block in range(blocks):
            q = h * blocks + block
            multiply_queued(q - 1)
            gather(gs[q % 2], h, block)
        idx_copy(2 * ahead + h, h).start()
        window_copy(2 * ahead + h, h).start()

    @pl.when(i == steps - 1)
    def _():
        multiply_queued(2 * blocks - 1)
        for h in range(2):
            idx_copy(2 * ahead + h, h).wait()
            window_copy(2 * ahead + h, h).wait()

        @pl.loop(0, out.shape[0])
        def _(d):
            for s in range(0, 16, 2):
                even = fill[d, s]
                odd = fill[d, s + 1]
                out[d, s // 2 : s // 2 + 1, :] = acc[pl.ds(even, 1), :]
                out[d, 8 + s // 2 : 9 + s // 2, :] = acc[pl.ds(odd, 1), :]
                ga[s : s + 1, :] = acc_tail[pl.ds(even, 1), :]
                ga[s + 1 : s + 2, :] = acc_tail[pl.ds(odd, 1), :]
            out[d, 16:24, :] = (
                ga[pl.ds(0, 8, stride=2), :]
                + pltpu.roll(ga[pl.ds(1, 8, stride=2), :], 64, axis=1)
                + labels[pl.ds(d, 8, stride=LANES), :]
            )


def m2l(idx, fill, own, recv, ops, labels, tb, kc, sends):
    terms = ops.shape[0]
    positions = ops.shape[1] // terms
    total = idx.shape[0] * idx.shape[1] // positions
    devices = fill.shape[0]
    cells_all = own.shape[0] // 2 + recv.shape[0] * sends
    width = (LANES - 1 + (kc - 1) * terms) // LANES * LANES + 3 * LANES
    return pl.pallas_call(
        functools.partial(m2l_kernel, tb, kc, sends, terms),
        grid=(positions // (2 * kc),),
        out_shape=jax.ShapeDtypeStruct((devices, 24, LANES), F32),
        in_specs=[
            hbm(),
            smem(),
            hbm(),
            pl.BlockSpec(recv.shape, lambda i: (0, 0, 0), pipeline_mode=pl.Buffered(1)),
            hbm(),
            pl.BlockSpec(labels.shape, lambda i: (0, 0), pipeline_mode=pl.Buffered(1)),
        ],
        out_specs=pl.BlockSpec((devices, 24, LANES), lambda i: (0, 0, 0)),
        scratch_shapes=[
            pltpu.VMEM((2 * cells_all, LANES), F32),
            pltpu.VMEM((total + 8, LANES), F32),
            pltpu.VMEM((total + 8, LANES), F32),
            pltpu.VMEM((2 * tb * kc, LANES), F32),
            pltpu.VMEM((2 * tb * kc, LANES), F32),
            pltpu.SMEM((total * kc,), I32),
            pltpu.SMEM((total * kc,), I32),
            pltpu.VMEM((terms, width), BF16),
            pltpu.VMEM((terms, width), BF16),
            pltpu.VMEM(((terms + 7) // 8 * 8, kc * 256), BF16),
            pltpu.VMEM(((terms + 7) // 8 * 8, kc * 256), BF16),
            pltpu.SemaphoreType.DMA((2,)),
            pltpu.SemaphoreType.DMA,
            pltpu.SemaphoreType.DMA((2,)),
        ],
        compiler_params=params(),
        name="m2l",
    )(idx, fill, own, recv, ops, labels)


def shift_of(k):
    return 2.0 * (k % 3 - 1), 2.0 * (k // 3 % 3 - 1), 2.0 * (k // 9 - 1)


FEATURES = 16


def pieces(x):
    high = x.astype(BF16)
    rest = x - high.astype(F32)
    middle = rest.astype(BF16)
    return high, middle, (rest - middle.astype(F32)).astype(BF16)


def near_kernel(per_step, neighbours, lists, targets, leaves, out, factors, *scratch):
    boxes_at_once = len(scratch) // 2
    mine, blocks = scratch[:boxes_at_once], scratch[boxes_at_once:]
    step = pl.program_id(0)
    count = leaves.shape[0] // 4

    def rows(r, n):
        return pl.ds(r, n, stride=FEATURES)

    @pl.when(step == 0)
    def _():
        parts = [leaves[pl.ds(c, count, stride=4), :] for c in range(3)]
        norm = parts[0] * parts[0] + parts[1] * parts[1] + parts[2] * parts[2]
        for c in range(3):
            factors[rows(c, count), :] = parts[c]
            factors[rows(3 + c, count), :] = parts[c]
        for p, piece in enumerate(pieces(norm)):
            factors[rows(6 + p, count), :] = piece.astype(F32)
        for r in range(9, FEATURES):
            factors[rows(r, count), :] = jnp.full((count, LANES), 1.0 if r < 12 else 0.0, F32)
        for u in range(boxes_at_once):
            blocks[u][...] = jnp.zeros_like(blocks[u])
            mine[u][...] = jnp.zeros_like(mine[u])
            for k in range(neighbours):
                for c, o in enumerate(shift_of(k)):
                    mine[u][FEATURES * k + 3 + c : FEATURES * k + 4 + c, :] = jnp.full((1, LANES), 2.0 * o, F32)
            for r in range(6, 9):
                mine[u][rows(r, neighbours), :] = jnp.ones((neighbours, LANES), F32)

    sub = lax.broadcasted_iota(I32, (neighbours, LANES), 0)
    shifts = [
        2.0 * (sub % 3 - 1).astype(F32),
        2.0 * (sub // 3 % 3 - 1).astype(F32),
        2.0 * (sub // 9 - 1).astype(F32),
    ]
    for u in range(per_step):
        slot = u % boxes_at_once
        near, wide = mine[slot], blocks[slot]
        norm = None
        for c in range(3):
            t = jnp.broadcast_to(targets[u, c : c + 1, :], (neighbours, LANES))
            near[rows(c, neighbours), :] = -2.0 * t
            d = t - shifts[c]
            norm = d * d if norm is None else norm + d * d
        for p, piece in enumerate(pieces(norm + SOFT_SQ)):
            near[rows(9 + p, neighbours), :] = piece.astype(F32)
        left = jnp.transpose(near[...]).astype(BF16)
        total = None
        for pair in range(neighbours // 2):
            masses = []
            for e in range(2):
                k = 2 * pair + e
                at = lists[(step * per_step + u) * neighbours + k]
                leaf = factors[pl.ds(pl.multiple_of(at * FEATURES, FEATURES), FEATURES), :]
                wide[FEATURES * k : FEATURES * (k + 1), LANES * k : LANES * (k + 1)] = leaf.astype(BF16)
                masses.append(leaves[pl.ds(at * 4 + 3, 1), :])
            square = jnp.dot(left, wide[:, 256 * pair : 256 * pair + 256], preferred_element_type=F32)
            for e in range(2):
                term = masses[e] * lax.rsqrt(square[:, LANES * e : LANES * (e + 1)])
                total = term if total is None else total + term
        out[u : u + 1, :] = jnp.sum(jnp.transpose(total), axis=0, keepdims=True)


def near_field(lists, targets, leaves):
    boxes = targets.shape[0]
    neighbours = lists.shape[0] // boxes
    count = leaves.shape[0] // 4
    per_step, at_once = 8, 4
    return pl.pallas_call(
        functools.partial(near_kernel, per_step, neighbours),
        grid=(boxes // per_step,),
        out_shape=jax.ShapeDtypeStruct((boxes, LANES), F32),
        in_specs=[
            smem(),
            pl.BlockSpec((per_step, 4, LANES), lambda i: (i, 0, 0)),
            pl.BlockSpec(leaves.shape, lambda i: (0, 0), pipeline_mode=pl.Buffered(1)),
        ],
        out_specs=pl.BlockSpec((per_step, LANES), lambda i: (i, 0)),
        scratch_shapes=[pltpu.VMEM((count * FEATURES, LANES), F32)]
        + [pltpu.VMEM((neighbours * FEATURES, LANES), F32)] * at_once
        + [pltpu.VMEM((neighbours * FEATURES, neighbours * LANES), BF16)] * at_once,
        compiler_params=params(),
        cost_estimate=pl.CostEstimate(flops=2**28, bytes_accessed=2**20, transcendentals=2**24),
        name="near",
    )(lists, targets, leaves)


def term_index(order):
    table = {}
    for degree in range(order + 1):
        for i in range(degree, -1, -1):
            for j in range(degree - i, -1, -1):
                table[(i, j, degree - i - j)] = len(table)
    return table


def final_kernel(order, arrived, coords, near, local, potential):
    sources = arrived.shape[0]
    rows = sources * 8
    tails = arrived[:, 16:24, :].reshape(rows, LANES)
    lane = lax.broadcasted_iota(I32, (rows, LANES), 1).astype(F32)
    sums = []
    for half in range(2):
        label = tails[:, 64 * half + LABEL : 64 * half + LABEL + 1]
        hot = jnp.where(lane == label, 1.0, 0.0).astype(BF16)
        body = arrived[:, 8 * half : 8 * half + 8, :].reshape(rows, LANES)
        both = jnp.concatenate([body, tails], axis=1)
        got = None
        for piece in pieces(both):
            part = lax.dot_general(hot, piece, (((0,), (0,)), ((), ())), preferred_element_type=F32)
            got = part if got is None else got + part
        sums.append(got)
    first = sums[0][:, 0:LANES] + sums[1][:, 0:LANES]
    rest = sums[0][:, LANES:256] + pltpu.roll(sums[1][:, LANES:256], 64, axis=1)
    local[:, 0:LANES] = first
    local[:, LANES : LANES + TAIL] = rest[:, 0:TAIL]
    terms = term_index(order)

    @pl.loop(0, local.shape[0] // 8)
    def _(g):
        box = pl.ds(pl.multiple_of(g * 8, 8), 8)
        head = local[box, 0:LANES]
        tail = local[box, LANES : LANES + TAIL]
        x, y, z = (coords[c, box, :] for c in range(3))

        def coefficient(i, j, m):
            a = terms[(i, j, m)]
            column = head[:, a : a + 1] if a < LANES else tail[:, a - LANES : a - LANES + 1]
            return jnp.broadcast_to(column, (8, LANES))

        in_z = None
        for m in range(order, -1, -1):
            in_y = None
            for j in range(order - m, -1, -1):
                in_x = None
                for i in range(order - m - j, -1, -1):
                    c = coefficient(i, j, m)
                    in_x = c if in_x is None else in_x * x + c
                in_y = in_x if in_y is None else in_y * y + in_x
            in_z = in_y if in_z is None else in_z * z + in_y
        potential[box, :] = in_z - near[box, :]


def finish(arrived, coords, near, terms):
    boxes = near.shape[0]
    return pl.pallas_call(
        functools.partial(final_kernel, ORDER),
        out_shape=(jax.ShapeDtypeStruct((boxes, terms), F32), jax.ShapeDtypeStruct((boxes, LANES), F32)),
        in_specs=[vmem(), vmem(), vmem()],
        out_specs=(vmem(), vmem()),
        compiler_params=params(),
        name="finish",
    )(arrived, coords, near)


def body(
    multipoles, positions, masses, m2l_ops, cell_sends, leaf_sends, m2l_lists, near_lists, owners, owner_boxes
):
    terms, own = multipoles.shape[3:]
    sections, sends = cell_sends.shape[3:]
    psends = leaf_sends.shape[4]
    total, positions_count = m2l_lists.shape[3:]
    boxes = positions.shape[3]
    bits = tuple((name, lax.axis_size(name).bit_length() - 1) for name in ("gx", "gy", "gz"))
    leaf_own = jnp.concatenate([positions[0, 0, 0], masses[0, 0, 0][:, None, :]], axis=1).astype(F32)
    send, own_rows, fill, labels = pick(
        cell_sends[0, 0, 0],
        leaf_sends[0, 0, 0],
        multipoles[0, 0, 0],
        leaf_own.reshape(boxes * 4, LANES),
        owners[0, 0, 0].reshape(1, total),
        owner_boxes[0, 0, 0].reshape(1, total),
    )
    recv = exchange(send, bits)
    tb, kc = 512, 2
    idx = jnp.transpose(m2l_lists[0, 0, 0]).reshape(positions_count // kc, kc, total // tb, tb)
    idx = 2 * jnp.transpose(idx, (0, 2, 1, 3)).reshape(positions_count // kc, kc * total)
    payload = m2l(idx, fill, own_rows, recv, m2l_ops, labels, tb, kc, sends)
    arrived = lax.all_to_all(payload, ("gx", "gy", "gz"), split_axis=0, concat_axis=0, tiled=True)
    got = recv[:, sends + sends // 3 :, :].astype(F32).reshape(sections * psends * 4, LANES)
    leaves = jnp.concatenate([leaf_own.reshape(boxes * 4, LANES), got], axis=0)
    near = near_field(near_lists[0, 0, 0].reshape(-1), leaf_own, leaves)
    coords = jnp.transpose(leaf_own[:, 0:3], (1, 0, 2))
    local, potential = finish(arrived, coords, near, terms)
    return local[None, None, None], potential[None, None, None]


def solution(mesh):
    five = P("gz", "gy", "gx", None, None)
    six = P("gz", "gy", "gx", None, None, None)
    return jax.shard_map(
        body,
        mesh=mesh,
        in_specs=(five, six, five, P(), five, five, five, five, five, P("gz", "gy", "gx", None)),
        out_specs=(five, five),
        check_vma=False,
    )
```

time: 231 us -> 199 us (0.86)
  Pallas kernels: 200 us -> 173 us
  other arithmetic: 7.18 us -> 2.86 us
  waiting for transfers between devices: 0.01 us -> 4.09 us
  local copies, waits for them, and re-layouts: 13.8 us -> 9.9 us
    pallas_call x3 -> x2, Pallas kernels: 170 us -> 138 us  [the longest x1 119 us: m2l(): pl.pallas_call(functools.partial(m2l_kernel, tb, kc, sends, terms), grid=...]
    pallas_call x1, Pallas kernels: 7.28 us -> 11.5 us  [pick(): pl.pallas_call(functools.partial(pick_kernel, sends, psends, sections), o...]
    all_to_all x1, waiting for transfers between devices: 0.01 us -> 4.09 us  [body(): lax.all_to_all(payload, ('gx', 'gy', 'gz'), split_axis=0, concat_axis=0,...]
    unnamed x12 -> x10, local copies, waits for them, and re-layouts: 3.99 us -> 5.48 us
  transfers between devices with their start and end apart: 1 -> 1, of which waited for: 0 -> 1; matrix products, arithmetic and copies ran while one was open for 1% -> 1% of each run, Pallas kernels for 18% -> 9%
where the time goes in v2:
time: 199 us; the launch traced here: 198 us
  Pallas kernels  173 us (87%)
  local copies, waits for them, and re-layouts  9.9 us (5%)
  starting transfers between devices  7.97 us (4%)
  waiting for transfers between devices  4.09 us (2%)
  other arithmetic  2.86 us (1%)
    pallas_call x1, Pallas kernels, m2l(): pl.pallas_call(functools.partial(m2l_kernel, tb, kc, sends, terms), grid=...  119 us
    pallas_call x1, Pallas kernels, near_field(): pl.pallas_call(functools.partial(near_kernel, per_step, neighbours), grid...  18.5 us
    pallas_call x1, Pallas kernels, exchange(): pl.pallas_call(functools.partial(exchange_kernel, bits), out_shape=jax.Sh...  14.2 us
    pallas_call x1, Pallas kernels, pick(): pl.pallas_call(functools.partial(pick_kernel, sends, psends, sections), o...  11.5 us
    pallas_call x1, Pallas kernels, finish(): pl.pallas_call(functools.partial(final_kernel, ORDER), out_shape=(jax.Sha...  9.12 us
    all_to_all x1, starting transfers between devices, body(): lax.all_to_all(payload, ('gx', 'gy', 'gz'), split_axis=0, concat_axis=0,...  7.97 us
    unnamed x10, local copies, waits for them, and re-layouts  5.48 us
    all_to_all x1, waiting for transfers between devices, body(): lax.all_to_all(payload, ('gx', 'gy', 'gz'), split_axis=0, concat_axis=0,...  4.09 us
  transfers between devices with their start and end apart: 1, of which 1 were waited for; matrix products, arithmetic and copies ran while one was open for 1% of the time, Pallas kernels for 9%

profile of v2, /device:TPU:1, one launch (start us, length us, event | category | flops | bytes accessed | tf_op | source)
XLA Modules:
  0.0 198.3 jit_solution(14838831201803227194)
XLA Ops:
  0.6 1.3 copy.26
  1.9 1.3 copy.25
  3.2 0.9 maximum_convert_fusion
  4.1 0.9 copy.17.targets
  5.0 1.1 multiply_bitcast_fusion
  6.1 0.2 copy.15
  6.3 0.4 mul.17
  6.8 0.3 copy.16
  7.1 1.2 mul.19.idx_hbm
  8.3 11.5 %pick.1 = (bf16[7,576,128]{2,1,0:T(8,128)(2,1)}, f32[2048,128]{1,0:T(8,128)}, s32[128,128]{1,0:T(8,128)}, f32[1024,128]{1,0:T(8,128)}) custom-call(s32[7,384]{1,0:T(8,128)} %bitcast.32, s32[7,16]{1,0:T(8,128)} %bitcast.34, bf16[165,1024]{1,0:T(8,128)(2,1)} %bitcast.29, f32[512,128]{1,0:T(8,128)} %bitcast.26, s32[1,1024]{1,0:T(1,128)} %bitcast.35, ...), custom_call_target="tpu_custom_call" | custom-call | tf_op jit(solution)/shard_map/pick/pallas_call | solution.py:98
  19.8 14.2 %exchange.1.recv = bf16[7,576,128]{2,1,0:T(8,128)(2,1)} custom-call(bf16[7,576,128]{2,1,0:T(8,128)(2,1)} %get-tuple-element.10.send), custom_call_target="tpu_custom_call" | custom-call | tf_op jit(solution)/shard_map/exchange/pallas_call | solution.py:149
  34.0 119.3 %m2l.1 = f32[128,24,128]{2,1,0:T(8,128)} custom-call(s32[64,2048]{1,0:T(8,128)} %mul.19.idx_hbm, s32[128,128]{1,0:T(8,128)} %get-tuple-element.8.fill, f32[2048,128]{1,0:T(8,128)} %get-tuple-element.9.own_hbm, bf16[7,576,128]{2,1,0:T(8,128)(2,1)} %exchange.1.recv, bf16[165,21120]{1,0:T(8,128)(2,1)} %ops_hbm.1, f32[1024,128]{1,0:T(8,128)} %get-tuple-element.11.labels), custom_call_target="tpu_custom_call" | custom-call | tf_op jit(solution)/shard_map/m2l/pallas_call | solution.py:290
  153.3 0.0 copy-start.2
  153.4 0.0 slice-start
  153.4 0.0 copy-start.1
  153.4 8.0 %all-to-all-start = ((f32[128,24,128]{2,1,0:T(8,128)}), f32[128,24,128]{2,1,0:T(8,128)S(1)}, u32[]{:S(2)}, u32[]{:S(2)}) async-start(f32[128,24,128]{2,1,0:T(8,128)} %m2l.1), calls=%async_computation | async-start | bytes 3145728 | tf_op jit(solution)/shard_map/all_to_all | solution.py:516
  161.4 0.0 copy-done.2
  161.4 0.1 copy.18
  161.5 0.7 reshape_squeeze.11.lists
  162.2 0.0 slice-done
  162.2 0.0 copy-done.1
  162.2 0.8 pad_maximum_fusion.leaves
  163.0 18.5 %near.1 = f32[128,128]{1,0:T(8,128)} custom-call(s32[1024]{0:T(1024)} %reshape_squeeze.11.lists, f32[128,4,128]{2,1,0:T(4,128)} %copy.17.targets, f32[960,128]{1,0:T(8,128)} %pad_maximum_fusion.leaves), custom_call_target="tpu_custom_call" | custom-call | flops 268435456 | bytes 1048576 | tf_op jit(solution)/shard_map/near/pallas_call | solution.py:406
  181.6 0.7 slice_bitcast_fusion.coords
  182.3 4.1 %all-to-all-done.arrived = f32[128,24,128]{2,1,0:T(8,128)S(1)} async-done(((f32[128,24,128]{2,1,0:T(8,128)}), f32[128,24,128]{2,1,0:T(8,128)S(1)}, u32[]{:S(2)}, u32[]{:S(2)}) %all-to-all-start) | async-done | bytes 1572896 | tf_op jit(solution)/shard_map/all_to_all | solution.py:516
  186.4 0.0 copy-start
  186.4 1.1 copy-done
  187.5 9.1 %finish.1 = (f32[128,165]{1,0:T(8,128)}, f32[128,128]{1,0:T(8,128)}) custom-call(f32[128,24,128]{2,1,0:T(8,128)} %copy-done, f32[3,128,128]{2,1,0:T(8,128)} %slice_bitcast_fusion.coords, f32[128,128]{1,0:T(8,128)} %near.1), custom_call_target="tpu_custom_call" | custom-call | tf_op jit(solution)/shard_map/finish/pallas_call | solution.py:483
  196.6 1.6 copy.20
  (1 shorter events, 0.0 us)
Async XLA Ops:
  153.3 8.0 %copy-start.2 = (s32[1,1,1,128,8]{3,4,2,1,0:T(8,128)S(1)}, s32[1,1,1,128,8]{3,4,2,1,0:T(8,128)}, u32[]{:S(2)}) copy-start(s32[1,1,1,128,8]{3,4,2,1,0:T(8,128)} %param.17) | copy-start | bytes 12292
  153.4 8.8 %slice-start = ((bf16[7,576,128]{2,1,0:T(8,128)(2,1)}), bf16[7,64,128]{2,1,0:T(8,128)(2,1)S(1)}, s32[]{:S(2)}) async-start(bf16[7,576,128]{2,1,0:T(8,128)(2,1)} %exchange.1.recv), calls=%async_computation.1 | async-start | bytes 229376 | tf_op jit(solution)/shard_map/slice | solution.py:517
  153.4 8.8 %copy-start.1 = (f32[128,4,128]{2,1,0:T(4,128)S(1)}, f32[128,4,128]{2,1,0:T(4,128)}, u32[]{:S(2)}) copy-start(f32[128,4,128]{2,1,0:T(4,128)} %copy.17.targets) | copy-start | bytes 786436
  153.4 33.0 %all-to-all-start = ((f32[128,24,128]{2,1,0:T(8,128)}), f32[128,24,128]{2,1,0:T(8,128)S(1)}, u32[]{:S(2)}, u32[]{:S(2)}) async-start(f32[128,24,128]{2,1,0:T(8,128)} %m2l.1), calls=%async_computation | async-start | bytes 3145728 | tf_op jit(solution)/shard_map/all_to_all | solution.py:516
  186.4 1.1 copy-start

commit v3 on v2

--- a/solution.py
+++ b/solution.py
@@ -33,28 +33,30 @@
     return pl.BlockSpec(memory_space=pl.ANY)
 
 
-def pick_kernel(sends, psends, sections, cell_idx, leaf_idx, terms, leaves, owner, box, out, pool, fill, labels, stage, leaf_stage):
+def pick_kernel(cell_idx, leaf_idx, terms, coords, masses, out, pool, stage, leaves, leaf_stage):
     count = terms.shape[1]
+    sections, _, sends = cell_idx.shape
+    psends = leaf_idx.shape[2]
+    boxes = masses.shape[0]
     for r in range(0, count, 256):
         first = jnp.transpose(terms[0:LANES, r : r + 256].astype(F32))
         rest = terms[LANES:, r : r + 256].astype(F32)
         pad = jnp.zeros((LANES - rest.shape[0], 256), F32)
         pool[pl.ds(2 * r, 256, stride=2), :] = first
         pool[pl.ds(2 * r + 1, 256, stride=2), :] = jnp.transpose(jnp.concatenate([rest, pad], axis=0))
+    for c in range(3):
+        leaves[pl.ds(c, boxes, stride=4), :] = coords[c].astype(F32)
+    leaves[pl.ds(3, boxes, stride=4), :] = masses[...].astype(F32)
 
     third = sends // 3
 
     @pl.loop(0, sections)
     def _(b):
-        @pl.loop(0, sends // 32)
-        def _(g):
-            for u in range(32):
-                r = g * 32 + u
-                c = cell_idx[b, r] * 2
-                stage[pl.ds(pl.multiple_of(2 * r, 2), 2), :] = pool[pl.ds(pl.multiple_of(c, 2), 2), :]
-
+        for r in range(sends):
+            c = cell_idx[b, 0, r] * 2
+            stage[2 * r : 2 * r + 2, :] = pool[pl.ds(pl.multiple_of(c, 2), 2), :]
         for u in range(psends):
-            c = leaf_idx[b, u] * 4
+            c = leaf_idx[b, 0, u] * 4
             leaf_stage[4 * u : 4 * u + 4, :] = leaves[pl.ds(pl.multiple_of(c, 4), 4), :]
         out[b, 0:sends, :] = stage[pl.ds(0, sends, stride=2), :].astype(BF16)
         tails = stage[pl.ds(1, third, stride=2), :]
@@ -63,6 +65,36 @@
         out[b, sends : sends + third, :] = tails.astype(BF16)
         out[b, sends + third : sends + third + 4 * psends, :] = leaf_stage[...].astype(BF16)
 
+
+def pick(cell_idx, leaf_idx, terms, coords, masses):
+    sections, _, sends = cell_idx.shape
+    psends = leaf_idx.shape[2]
+    boxes = masses.shape[0]
+    width = sends + sends // 3 + 4 * psends
+    return pl.pallas_call(
+        pick_kernel,
+        out_shape=(
+            jax.ShapeDtypeStruct((sections, width, LANES), BF16),
+            jax.ShapeDtypeStruct((2 * terms.shape[1], LANES), F32),
+        ),
+        in_specs=[smem(), smem(), vmem(), vmem(), vmem()],
+        out_specs=(vmem(), vmem()),
+        scratch_shapes=[
+            pltpu.VMEM((2 * sends, LANES), F32),
+            pltpu.VMEM((4 * boxes, LANES), F32),
+            pltpu.VMEM((4 * psends, LANES), F32),
+        ],
+        compiler_params=params(),
+        name="pick",
+    )(cell_idx, leaf_idx, terms, coords, masses)
+
+
+def flip(index, bit):
+    step = 1 << bit
+    return index + step - 2 * step * (index // step % 2)
+
+
+def fill_slots(owner, box, fill, labels):
     rows = owner.shape[1]
     line = lax.broadcasted_iota(I32, (LANES, rows), 0)
     rank_of_line = line // 32 + line // 8 % 4 * 4 + line % 8 * 16
@@ -70,13 +102,13 @@
     hot16 = hot.astype(BF16)
     sooner = lax.broadcasted_iota(I32, (rows, rows), 0) < lax.broadcasted_iota(I32, (rows, rows), 1)
     earlier = jnp.dot(hot16, jnp.where(sooner, 1.0, 0.0).astype(BF16), preferred_element_type=F32)
-    rank = jnp.sum(earlier * hot, axis=0, keepdims=True).astype(I32)
+    rank = jnp.sum(earlier * hot, axis=0, keepdims=True)
     row = lax.broadcasted_iota(I32, (LANES, rows), 1)
     kind = line // 16
     value = jnp.where(
         kind == 0, row // 32, jnp.where(kind == 1, row % 32, jnp.where(kind == 2, box[...], jnp.where(kind == 3, 1, 0)))
     )
-    value = jnp.where(line % 16 == rank, value, 0).astype(F32).astype(BF16)
+    value = jnp.where((line % 16).astype(F32) == rank, value.astype(F32), 0.0).astype(BF16)
     slots = lax.dot_general(hot16, value, (((1,), (1,)), ((), ())), preferred_element_type=F32)
     used = pltpu.roll(slots, LANES - 48, axis=1) > 0.5
     at = slots * 32.0 + pltpu.roll(slots, LANES - 16, axis=1)
@@ -91,35 +123,19 @@
         )
 
 
-def pick(cell_idx, leaf_idx, terms, leaves, owner, box):
-    sections, sends = cell_idx.shape
-    psends = leaf_idx.shape[1]
-    width = sends + sends // 3 + 4 * psends
-    return pl.pallas_call(
-        functools.partial(pick_kernel, sends, psends, sections),
-        out_shape=(
-            jax.ShapeDtypeStruct((sections, width, LANES), BF16),
-            jax.ShapeDtypeStruct((2 * terms.shape[1], LANES), F32),
-            jax.ShapeDtypeStruct((LANES, LANES), I32),
-            jax.ShapeDtypeStruct((8 * LANES, LANES), F32),
-        ),
-        in_specs=[smem(), smem(), vmem(), vmem(), vmem(), vmem()],
-        out_specs=(vmem(),) * 4,
-        scratch_shapes=[
-            pltpu.VMEM((2 * sends, LANES), F32),
-            pltpu.VMEM((4 * psends, LANES), F32),
-        ],
-        compiler_params=params(),
-        name="pick",
-    )(cell_idx, leaf_idx, terms, leaves, owner, box)
-
-
-def flip(index, bit):
-    step = 1 << bit
-    return index + step - 2 * step * (index // step % 2)
-
-
-def exchange_kernel(bits, send, recv, send_sem, recv_sem):
+def order_lists(tb, kc, lists, idx, turned):
+    total, positions = lists.shape
+    for t in range(0, total, LANES):
+        turned[...] = jnp.transpose(lists[t : t + LANES, :].astype(F32))
+        for kk in range(kc):
+            at = t // tb * kc * tb + kk * tb + t % tb
+            part = turned[pl.ds(kk, positions // kc, stride=kc), :]
+            idx[:, at : at + LANES] = (2.0 * part).astype(I32)
+
+
+def exchange_kernel(
+    bits, tb, kc, send, owner, box, lists, recv, fill, labels, idx, turned, send_sem, recv_sem
+):
     partners = []
     for name, count in bits:
         for bit in range(count):
@@ -140,21 +156,33 @@
         )
         copy.start()
         copies.append(copy)
+    order_lists(tb, kc, lists, idx, turned)
+    fill_slots(owner, box, fill, labels)
     for copy in copies:
         copy.wait()
 
 
-def exchange(send, bits):
+def exchange(send, owner, box, lists, bits, tb, kc):
     sections = send.shape[0]
+    total, positions = lists.shape
     return pl.pallas_call(
-        functools.partial(exchange_kernel, bits),
-        out_shape=jax.ShapeDtypeStruct(send.shape, send.dtype),
-        in_specs=[hbm()],
-        out_specs=hbm(),
-        scratch_shapes=[pltpu.SemaphoreType.DMA((sections,)), pltpu.SemaphoreType.DMA((sections,))],
-        compiler_params=pltpu.CompilerParams(collective_id=0, has_side_effects=True),
+        functools.partial(exchange_kernel, bits, tb, kc),
+        out_shape=(
+            jax.ShapeDtypeStruct(send.shape, send.dtype),
+            jax.ShapeDtypeStruct((LANES, LANES), I32),
+            jax.ShapeDtypeStruct((8 * LANES, LANES), F32),
+            jax.ShapeDtypeStruct((positions // kc, kc * total), I32),
+        ),
+        in_specs=[hbm(), vmem(), vmem(), vmem()],
+        out_specs=(hbm(), vmem(), vmem(), vmem()),
+        scratch_shapes=[
+            pltpu.VMEM((positions, LANES), F32),
+            pltpu.SemaphoreType.DMA((sections,)),
+            pltpu.SemaphoreType.DMA((sections,)),
+        ],
+        compiler_params=params(collective_id=0, has_side_effects=True),
         name="exchange",
-    )(send)
+    )(send, owner, box, lists)
 
 
 def m2l_kernel(
@@ -335,7 +363,7 @@
     return high, middle, (rest - middle.astype(F32)).astype(BF16)
 
 
-def near_kernel(per_step, neighbours, lists, targets, leaves, out, factors, *scratch):
+def near_kernel(per_step, neighbours, lists, coords, own_mass, got, out, leaves, factors, *scratch):
     boxes_at_once = len(scratch) // 2
     mine, blocks = scratch[:boxes_at_once], scratch[boxes_at_once:]
     step = pl.program_id(0)
@@ -346,6 +374,13 @@
 
     @pl.when(step == 0)
     def _():
+        boxes = own_mass.shape[0]
+        for c in range(3):
+            leaves[pl.ds(c, boxes, stride=4), :] = coords[c].astype(F32)
+        leaves[pl.ds(3, boxes, stride=4), :] = own_mass[...].astype(F32)
+        for b in range(got.shape[0]):
+            at = 4 * boxes + b * got.shape[1]
+            leaves[at : at + got.shape[1], :] = got[b].astype(F32)
         parts = [leaves[pl.ds(c, count, stride=4), :] for c in range(3)]
         norm = parts[0] * parts[0] + parts[1] * parts[1] + parts[2] * parts[2]
         for c in range(3):
@@ -375,7 +410,7 @@
         near, wide = mine[slot], blocks[slot]
         norm = None
         for c in range(3):
-            t = jnp.broadcast_to(targets[u, c : c + 1, :], (neighbours, LANES))
+            t = jnp.broadcast_to(leaves[pl.ds(4 * (step * per_step + u) + c, 1), :], (neighbours, LANES))
             near[rows(c, neighbours), :] = -2.0 * t
             d = t - shifts[c]
             norm = d * d if norm is None else norm + d * d
@@ -387,7 +422,7 @@
             masses = []
             for e in range(2):
                 k = 2 * pair + e
-                at = lists[(step * per_step + u) * neighbours + k]
+                at = lists[k, step * per_step + u]
                 leaf = factors[pl.ds(pl.multiple_of(at * FEATURES, FEATURES), FEATURES), :]
                 wide[FEATURES * k : FEATURES * (k + 1), LANES * k : LANES * (k + 1)] = leaf.astype(BF16)
                 masses.append(leaves[pl.ds(at * 4 + 3, 1), :])
@@ -398,10 +433,11 @@
         out[u : u + 1, :] = jnp.sum(jnp.transpose(total), axis=0, keepdims=True)
 
 
-def near_field(lists, targets, leaves):
-    boxes = targets.shape[0]
-    neighbours = lists.shape[0] // boxes
-    count = leaves.shape[0] // 4
+def near_field(lists, coords, masses, recv, psends):
+    neighbours, boxes = lists.shape
+    sections, width, _ = recv.shape
+    tail = 4 * psends
+    count = boxes + sections * psends
     per_step, at_once = 8, 4
     return pl.pallas_call(
         functools.partial(near_kernel, per_step, neighbours),
@@ -409,17 +445,18 @@
         out_shape=jax.ShapeDtypeStruct((boxes, LANES), F32),
         in_specs=[
             smem(),
-            pl.BlockSpec((per_step, 4, LANES), lambda i: (i, 0, 0)),
-            pl.BlockSpec(leaves.shape, lambda i: (0, 0), pipeline_mode=pl.Buffered(1)),
+            pl.BlockSpec(coords.shape, lambda i: (0, 0, 0), pipeline_mode=pl.Buffered(1)),
+            pl.BlockSpec(masses.shape, lambda i: (0, 0), pipeline_mode=pl.Buffered(1)),
+            pl.BlockSpec((sections, tail, LANES), lambda i: (0, width // tail - 1, 0), pipeline_mode=pl.Buffered(1)),
         ],
         out_specs=pl.BlockSpec((per_step, LANES), lambda i: (i, 0)),
-        scratch_shapes=[pltpu.VMEM((count * FEATURES, LANES), F32)]
+        scratch_shapes=[pltpu.VMEM((count * 4, LANES), F32), pltpu.VMEM((count * FEATURES, LANES), F32)]
         + [pltpu.VMEM((neighbours * FEATURES, LANES), F32)] * at_once
         + [pltpu.VMEM((neighbours * FEATURES, neighbours * LANES), BF16)] * at_once,
         compiler_params=params(),
         cost_estimate=pl.CostEstimate(flops=2**28, bytes_accessed=2**20, transcendentals=2**24),
         name="near",
-    )(lists, targets, leaves)
+    )(lists, coords, masses, recv)
 
 
 def term_index(order):
@@ -431,61 +468,62 @@
     return table
 
 
-def final_kernel(order, arrived, coords, near, local, potential):
+def final_kernel(order, arrived, coords, near, local, potential, rows_of_terms):
     sources = arrived.shape[0]
     rows = sources * 8
+    boxes = near.shape[0]
     tails = arrived[:, 16:24, :].reshape(rows, LANES)
-    lane = lax.broadcasted_iota(I32, (rows, LANES), 1).astype(F32)
-    sums = []
+    turned = jnp.transpose(tails)
+    line = lax.broadcasted_iota(I32, (boxes, rows), 0).astype(F32)
+    hots = []
     for half in range(2):
-        label = tails[:, 64 * half + LABEL : 64 * half + LABEL + 1]
-        hot = jnp.where(lane == label, 1.0, 0.0).astype(BF16)
-        body = arrived[:, 8 * half : 8 * half + 8, :].reshape(rows, LANES)
-        both = jnp.concatenate([body, tails], axis=1)
-        got = None
-        for piece in pieces(both):
-            part = lax.dot_general(hot, piece, (((0,), (0,)), ((), ())), preferred_element_type=F32)
-            got = part if got is None else got + part
-        sums.append(got)
-    first = sums[0][:, 0:LANES] + sums[1][:, 0:LANES]
-    rest = sums[0][:, LANES:256] + pltpu.roll(sums[1][:, LANES:256], 64, axis=1)
-    local[:, 0:LANES] = first
-    local[:, LANES : LANES + TAIL] = rest[:, 0:TAIL]
+        label = turned[64 * half + LABEL : 64 * half + LABEL + 1, :]
+        hots.append(jnp.where(line == label, 1.0, 0.0).astype(BF16))
+    first = None
+    for half in range(2):
+        for piece in pieces(arrived[:, 8 * half : 8 * half + 8, :].reshape(rows, LANES)):
+            part = jnp.dot(hots[half], piece, preferred_element_type=F32)
+            first = part if first is None else first + part
+    both = None
+    hot = jnp.concatenate(hots, axis=0)
+    for piece in pieces(tails):
+        part = jnp.dot(hot, piece, preferred_element_type=F32)
+        both = part if both is None else both + part
+    rest = both[0:boxes] + pltpu.roll(both[boxes:], 64, axis=1)
+    rows_of_terms[0:LANES, :] = jnp.transpose(first)
+    rows_of_terms[LANES:, :] = jnp.transpose(rest)
+    for a in range(LANES + TAIL):
+        local[a] = rows_of_terms[a : a + 1, :]
     terms = term_index(order)
-
-    @pl.loop(0, local.shape[0] // 8)
-    def _(g):
-        box = pl.ds(pl.multiple_of(g * 8, 8), 8)
-        head = local[box, 0:LANES]
-        tail = local[box, LANES : LANES + TAIL]
-        x, y, z = (coords[c, box, :] for c in range(3))
-
-        def coefficient(i, j, m):
-            a = terms[(i, j, m)]
-            column = head[:, a : a + 1] if a < LANES else tail[:, a - LANES : a - LANES + 1]
-            return jnp.broadcast_to(column, (8, LANES))
-
+    x, y, z = (jnp.transpose(coords[c].astype(F32)) for c in range(3))
+    step = 32
+    parts = []
+    for p in range(0, LANES, step):
+        xs, ys, zs = x[p : p + step], y[p : p + step], z[p : p + step]
         in_z = None
         for m in range(order, -1, -1):
             in_y = None
             for j in range(order - m, -1, -1):
                 in_x = None
                 for i in range(order - m - j, -1, -1):
-                    c = coefficient(i, j, m)
-                    in_x = c if in_x is None else in_x * x + c
-                in_y = in_x if in_y is None else in_y * y + in_x
-            in_z = in_y if in_z is None else in_z * z + in_y
-        potential[box, :] = in_z - near[box, :]
+                    a = terms[(i, j, m)]
+                    c = rows_of_terms[a : a + 1, :]
+                    in_x = jnp.broadcast_to(c, xs.shape) if in_x is None else in_x * xs + c
+                in_y = in_x if in_y is None else in_y * ys + in_x
+            in_z = in_y if in_z is None else in_z * zs + in_y
+        parts.append(in_z)
+    potential[...] = jnp.transpose(jnp.concatenate(parts, axis=0)) - near[...]
 
 
 def finish(arrived, coords, near, terms):
     boxes = near.shape[0]
     return pl.pallas_call(
         functools.partial(final_kernel, ORDER),
-        out_shape=(jax.ShapeDtypeStruct((boxes, terms), F32), jax.ShapeDtypeStruct((boxes, LANES), F32)),
+        out_shape=(jax.ShapeDtypeStruct((terms, 1, boxes), F32), jax.ShapeDtypeStruct((boxes, LANES), F32)),
         in_specs=[vmem(), vmem(), vmem()],
         out_specs=(vmem(), vmem()),
-        compiler_params=params(),
+        scratch_shapes=[pltpu.VMEM((2 * LANES, LANES), F32)],
+        compiler_params=pltpu.CompilerParams(vmem_limit_bytes=24 * 2**20),
         name="finish",
     )(arrived, coords, near)
 
@@ -496,30 +534,28 @@
     terms, own = multipoles.shape[3:]
     sections, sends = cell_sends.shape[3:]
     psends = leaf_sends.shape[4]
-    total, positions_count = m2l_lists.shape[3:]
-    boxes = positions.shape[3]
+    total = m2l_lists.shape[3]
     bits = tuple((name, lax.axis_size(name).bit_length() - 1) for name in ("gx", "gy", "gz"))
-    leaf_own = jnp.concatenate([positions[0, 0, 0], masses[0, 0, 0][:, None, :]], axis=1).astype(F32)
-    send, own_rows, fill, labels = pick(
-        cell_sends[0, 0, 0],
-        leaf_sends[0, 0, 0],
-        multipoles[0, 0, 0],
-        leaf_own.reshape(boxes * 4, LANES),
+    coords = jnp.transpose(positions[0, 0, 0], (1, 0, 2))
+    mass = masses[0, 0, 0]
+    send, own_rows = pick(
+        cell_sends[0, 0, 0][:, None, :], leaf_sends[0, 0, 0][:, None, :], multipoles[0, 0, 0], coords, mass
+    )
+    tb, kc = 512, 2
+    recv, fill, labels, idx = exchange(
+        send,
         owners[0, 0, 0].reshape(1, total),
         owner_boxes[0, 0, 0].reshape(1, total),
+        m2l_lists[0, 0, 0],
+        bits,
+        tb,
+        kc,
     )
-    recv = exchange(send, bits)
-    tb, kc = 512, 2
-    idx = jnp.transpose(m2l_lists[0, 0, 0]).reshape(positions_count // kc, kc, total // tb, tb)
-    idx = 2 * jnp.transpose(idx, (0, 2, 1, 3)).reshape(positions_count // kc, kc * total)
     payload = m2l(idx, fill, own_rows, recv, m2l_ops, labels, tb, kc, sends)
     arrived = lax.all_to_all(payload, ("gx", "gy", "gz"), split_axis=0, concat_axis=0, tiled=True)
-    got = recv[:, sends + sends // 3 :, :].astype(F32).reshape(sections * psends * 4, LANES)
-    leaves = jnp.concatenate([leaf_own.reshape(boxes * 4, LANES), got], axis=0)
-    near = near_field(near_lists[0, 0, 0].reshape(-1), leaf_own, leaves)
-    coords = jnp.transpose(leaf_own[:, 0:3], (1, 0, 2))
+    near = near_field(jnp.transpose(near_lists[0, 0, 0]), coords, mass, recv, psends)
     local, potential = finish(arrived, coords, near, terms)
-    return local[None, None, None], potential[None, None, None]
+    return jnp.transpose(local[None, None], (0, 1, 3, 4, 2)), potential[None, None, None]
 
 
 def solution(mesh):

time: 199 us -> 179 us (0.90)
  Pallas kernels: 173 us -> 163 us
  local copies, waits for them, and re-layouts: 9.9 us -> 0.85 us
  other arithmetic: 2.86 us -> 0 us
  waiting for transfers between devices: 4.09 us -> 6.19 us
    pallas_call x1, Pallas kernels: 9.12 us -> 2.69 us  [finish(): pl.pallas_call(functools.partial(final_kernel, ORDER), out_shape=(jax.Sha...]
    unnamed x10 -> x4, local copies, waits for them, and re-layouts: 5.48 us -> 0.85 us
    pallas_call x2, Pallas kernels: 25.7 us -> 22.3 us  [the longest x1 16.3 us: exchange(): pl.pallas_call(functools.partial(exchange_kernel, bits, tb, kc), out_shap...]
    mul x4 -> x0, local copies, waits for them, and re-layouts: 2.14 us -> none  [body(): 2 * jnp.transpose(idx, (0, 2, 1, 3)).reshape(positions_count // kc, kc *...]
    all_to_all x1, waiting for transfers between devices: 4.09 us -> 6.19 us  [body(): lax.all_to_all(payload, ('gx', 'gy', 'gz'), split_axis=0, concat_axis=0,...]
  transfers between devices with their start and end apart: 1 -> 1, of which waited for: 1 -> 1; matrix products, arithmetic and copies ran while one was open for 1% -> 0% of each run, Pallas kernels for 9% -> 11%
where the time goes in v3:
time: 179 us
  Pallas kernels  163 us (91%)
  starting transfers between devices  7.93 us (4%)
  waiting for transfers between devices  6.19 us (3%)
    pallas_call x1, Pallas kernels, m2l(): pl.pallas_call(functools.partial(m2l_kernel, tb, kc, sends, terms), grid=...  119 us
    pallas_call x1, Pallas kernels, near_field(): pl.pallas_call(functools.partial(near_kernel, per_step, neighbours), grid...  18.8 us
    pallas_call x1, Pallas kernels, exchange(): pl.pallas_call(functools.partial(exchange_kernel, bits, tb, kc), out_shap...  16.3 us
    all_to_all x1, starting transfers between devices, body(): lax.all_to_all(payload, ('gx', 'gy', 'gz'), split_axis=0, concat_axis=0,...  7.93 us
    all_to_all x1, waiting for transfers between devices, body(): lax.all_to_all(payload, ('gx', 'gy', 'gz'), split_axis=0, concat_axis=0,...  6.19 us
    pallas_call x1, Pallas kernels, pick(): pl.pallas_call(pick_kernel, out_shape=(jax.ShapeDtypeStruct((sections, wi...  5.94 us
  transfers between devices with their start and end apart: 1, of which 1 were waited for; matrix products, arithmetic and copies ran while one was open for 0% of the time, Pallas kernels for 11%

profile of v3, /device:TPU:1, one launch (start us, length us, event | category | flops | bytes accessed | tf_op | source)
XLA Modules:
  0.0 178.7 jit_solution(11890296644676332398)
XLA Ops:
  0.6 5.9 %pick.1 = (bf16[7,576,128]{2,1,0:T(8,128)(2,1)}, f32[2048,128]{1,0:T(8,128)}) custom-call(s32[7,1,384]{2,1,0:T(1,128)} %bitcast.24, s32[7,1,16]{2,1,0:T(1,128)} %bitcast.27, bf16[165,1024]{1,0:T(8,128)(2,1)} %bitcast.21, bf16[3,128,128]{2,1,0:T(8,128)(2,1)} %bitcast.17, bf16[128,128]{1,0:T(8,128)(2,1)} %bitcast.22), custom_call_target="tpu_custom_call" | custom-call | tf_op jit(solution)/shard_map/pick/pallas_call | solution.py:74
  6.6 16.3 %exchange.1 = (bf16[7,576,128]{2,1,0:T(8,128)(2,1)}, s32[128,128]{1,0:T(8,128)}, f32[1024,128]{1,0:T(8,128)}, s32[64,2048]{1,0:T(8,128)}) custom-call(bf16[7,576,128]{2,1,0:T(8,128)(2,1)} %get-tuple-element.10.send, s32[1,1024]{1,0:T(1,128)} %bitcast.25, s32[1,1024]{1,0:T(1,128)} %bitcast.26, s32[1024,128]{1,0:T(8,128)} %bitcast.20), custom_call_target="tpu_custom_call" | custom-call | tf_op jit(solution)/shard_map/exchange/pallas_call | solution.py:168
  22.9 119.3 %m2l.1 = f32[128,24,128]{2,1,0:T(8,128)} custom-call(s32[64,2048]{1,0:T(8,128)} %get-tuple-element.11.idx_hbm, s32[128,128]{1,0:T(8,128)} %get-tuple-element.12.fill, f32[2048,128]{1,0:T(8,128)} %get-tuple-element.13.own_hbm, bf16[7,576,128]{2,1,0:T(8,128)(2,1)} %get-tuple-element.14.recv.got, bf16[165,21120]{1,0:T(8,128)(2,1)} %ops_hbm.1, ...), custom_call_target="tpu_custom_call" | custom-call | tf_op jit(solution)/shard_map/m2l/pallas_call | solution.py:318
  142.3 7.9 %all-to-all-start = ((f32[128,24,128]{2,1,0:T(8,128)}), f32[128,24,128]{2,1,0:T(8,128)S(1)}, u32[]{:S(2)}, u32[]{:S(2)}) async-start(f32[128,24,128]{2,1,0:T(8,128)} %m2l.1), calls=%async_computation | async-start | bytes 3145728 | tf_op jit(solution)/shard_map/all_to_all | solution.py:555
  150.2 0.0 copy-start
  150.2 18.8 %near.1 = f32[128,128]{1,0:T(8,128)} custom-call(s32[8,128]{1,0:T(8,128)} %bitcast.30, bf16[3,128,128]{2,1,0:T(8,128)(2,1)} %bitcast.18, bf16[128,128]{1,0:T(8,128)(2,1)} %bitcast.23, bf16[7,576,128]{2,1,0:T(8,128)(2,1)} %get-tuple-element.14.recv.got), custom_call_target="tpu_custom_call" | custom-call | flops 268435456 | bytes 1048576 | tf_op jit(solution)/shard_map/near/pallas_call | solution.py:442
  169.0 6.2 %all-to-all-done.arrived = f32[128,24,128]{2,1,0:T(8,128)S(1)} async-done(((f32[128,24,128]{2,1,0:T(8,128)}), f32[128,24,128]{2,1,0:T(8,128)S(1)}, u32[]{:S(2)}, u32[]{:S(2)}) %all-to-all-start) | async-done | bytes 1572896 | tf_op jit(solution)/shard_map/all_to_all | solution.py:555
  175.2 0.0 copy-done
  175.2 0.0 copy-start.1
  175.2 0.8 copy-done.1
  176.1 2.7 %finish.1 = (f32[165,1,128]{2,1,0:T(1,128)}, f32[128,128]{1,0:T(8,128)}) custom-call(f32[128,24,128]{2,1,0:T(8,128)S(1)} %all-to-all-done.arrived, bf16[3,128,128]{2,1,0:T(8,128)(2,1)S(1)} %bitcast.19, f32[128,128]{1,0:T(8,128)S(1)} %copy-done.1), custom_call_target="tpu_custom_call" | custom-call | tf_op jit(solution)/shard_map/finish/pallas_call | solution.py:520
Async XLA Ops:
  142.3 32.9 %all-to-all-start = ((f32[128,24,128]{2,1,0:T(8,128)}), f32[128,24,128]{2,1,0:T(8,128)S(1)}, u32[]{:S(2)}, u32[]{:S(2)}) async-start(f32[128,24,128]{2,1,0:T(8,128)} %m2l.1), calls=%async_computation | async-start | bytes 3145728 | tf_op jit(solution)/shard_map/all_to_all | solution.py:555
  150.2 25.0 %copy-start = (bf16[1,1,1,128,3,128]{5,3,4,2,1,0:T(8,128)(2,1)S(1)}, bf16[1,1,1,128,3,128]{5,3,4,2,1,0:T(8,128)(2,1)}, u32[]{:S(2)}) copy-start(bf16[1,1,1,128,3,128]{5,3,4,2,1,0:T(8,128)(2,1)} %param.11) | copy-start | bytes 294916
  175.2 0.8 copy-start.1

commit v4 on v3

--- a/solution.py
+++ b/solution.py
@@ -112,11 +112,11 @@
     slots = lax.dot_general(hot16, value, (((1,), (1,)), ((), ())), preferred_element_type=F32)
     used = pltpu.roll(slots, LANES - 48, axis=1) > 0.5
     at = slots * 32.0 + pltpu.roll(slots, LANES - 16, axis=1)
-    fill[...] = jnp.where(used, at, float(rows)).astype(I32)
+    fill[...] = jnp.transpose(jnp.where(used, at, float(rows)))[0:16].astype(I32)
     label = jnp.where(used, pltpu.roll(slots, LANES - 32, axis=1), -1.0)
     lane = lax.broadcasted_iota(I32, (LANES, LANES), 1)
     for j in range(8):
-        labels[j * LANES : (j + 1) * LANES, :] = jnp.where(
+        labels[pl.ds(j, LANES, stride=8), :] = jnp.where(
             lane == LABEL,
             label[:, 2 * j : 2 * j + 1],
             jnp.where(lane == 64 + LABEL, label[:, 2 * j + 1 : 2 * j + 2], 0.0),
@@ -169,7 +169,7 @@
         functools.partial(exchange_kernel, bits, tb, kc),
         out_shape=(
             jax.ShapeDtypeStruct(send.shape, send.dtype),
-            jax.ShapeDtypeStruct((LANES, LANES), I32),
+            jax.ShapeDtypeStruct((16, LANES), I32),
             jax.ShapeDtypeStruct((8 * LANES, LANES), F32),
             jax.ShapeDtypeStruct((positions // kc, kc * total), I32),
         ),
@@ -187,9 +187,10 @@
 
 def m2l_kernel(
     tb, kc, sends, terms, idx_hbm, fill, own_hbm, recv, ops_hbm, labels, out,
-    pool, acc, acc_tail, ga, gb, idx_a, idx_b, window_a, window_b, panel_a, panel_b, sem, own_sem, window_sem,
+    pools, acc_box, tail_box, ga, gb, idx_a, idx_b, window_a, window_b, panel_a, panel_b, sem, own_sem, window_sem,
 ):
-    total = acc.shape[0] - 8
+    acc, acc_tail = acc_box.at[0], tail_box.at[0]
+    total = acc_box.shape[1] - 8
     blocks = total // tb
     chunk = tb * kc
     gs, idxs = (ga, gb), (idx_a, idx_b)
@@ -227,10 +228,14 @@
             panels[h][0:terms, u * 256 : u * 256 + LANES] = first.astype(BF16)
             panels[h][0:terms, u * 256 + LANES : u * 256 + 256] = second.astype(BF16)
 
+    first = jnp.minimum(i, 0)
+    rows = pools.at[first]
+    pool = pools.at[0]
+
     def gather(g, h, block):
         for r in range(chunk):
             c = idxs[h][block * chunk + r]
-            g[2 * r : 2 * r + 2, :] = pool[pl.ds(pl.multiple_of(c, 2), 2), :]
+            g[2 * r : 2 * r + 2, :] = rows[pl.ds(pl.multiple_of(c, 2), 2), :]
 
     def multiply(g, block, panel):
         parts = []
@@ -292,19 +297,20 @@
             idx_copy(2 * ahead + h, h).wait()
             window_copy(2 * ahead + h, h).wait()
 
-        @pl.loop(0, out.shape[0])
-        def _(d):
+        heads, ends = acc_box.at[first], tail_box.at[first]
+        for d in range(out.shape[0]):
+            base = d % 32 * 16
             for s in range(0, 16, 2):
-                even = fill[d, s]
-                odd = fill[d, s + 1]
-                out[d, s // 2 : s // 2 + 1, :] = acc[pl.ds(even, 1), :]
-                out[d, 8 + s // 2 : 9 + s // 2, :] = acc[pl.ds(odd, 1), :]
-                ga[s : s + 1, :] = acc_tail[pl.ds(even, 1), :]
-                ga[s + 1 : s + 2, :] = acc_tail[pl.ds(odd, 1), :]
+                even = fill[s, d]
+                odd = fill[s + 1, d]
+                out[d, s // 2 : s // 2 + 1, :] = heads[pl.ds(even, 1), :]
+                out[d, 8 + s // 2 : 9 + s // 2, :] = heads[pl.ds(odd, 1), :]
+                ga[base + s : base + s + 1, :] = ends[pl.ds(even, 1), :]
+                ga[base + s + 1 : base + s + 2, :] = ends[pl.ds(odd, 1), :]
             out[d, 16:24, :] = (
-                ga[pl.ds(0, 8, stride=2), :]
-                + pltpu.roll(ga[pl.ds(1, 8, stride=2), :], 64, axis=1)
-                + labels[pl.ds(d, 8, stride=LANES), :]
+                ga[pl.ds(base, 8, stride=2), :]
+                + pltpu.roll(ga[pl.ds(base + 1, 8, stride=2), :], 64, axis=1)
+                + labels[8 * d : 8 * d + 8, :]
             )
 
 
@@ -312,7 +318,7 @@
     terms = ops.shape[0]
     positions = ops.shape[1] // terms
     total = idx.shape[0] * idx.shape[1] // positions
-    devices = fill.shape[0]
+    devices = fill.shape[1]
     cells_all = own.shape[0] // 2 + recv.shape[0] * sends
     width = (LANES - 1 + (kc - 1) * terms) // LANES * LANES + 3 * LANES
     return pl.pallas_call(
@@ -329,9 +335,9 @@
         ],
         out_specs=pl.BlockSpec((devices, 24, LANES), lambda i: (0, 0, 0)),
         scratch_shapes=[
-            pltpu.VMEM((2 * cells_all, LANES), F32),
-            pltpu.VMEM((total + 8, LANES), F32),
-            pltpu.VMEM((total + 8, LANES), F32),
+            pltpu.VMEM((1, 2 * cells_all, LANES), F32),
+            pltpu.VMEM((1, total + 8, LANES), F32),
+            pltpu.VMEM((1, total + 8, LANES), F32),
             pltpu.VMEM((2 * tb * kc, LANES), F32),
             pltpu.VMEM((2 * tb * kc, LANES), F32),
             pltpu.SMEM((total * kc,), I32),

time: 179 us -> 170 us (0.950)
  Pallas kernels: 163 us -> 154 us
    pallas_call x1, Pallas kernels: 119 us -> 110 us  [m2l(): pl.pallas_call(functools.partial(m2l_kernel, tb, kc, sends, terms), grid=...]
where the time goes in v4:
time: 170 us; the launch traced here: 169 us
  Pallas kernels  154 us (91%)
  starting transfers between devices  7.95 us (5%)
  waiting for transfers between devices  6.19 us (4%)
    pallas_call x1, Pallas kernels, m2l(): pl.pallas_call(functools.partial(m2l_kernel, tb, kc, sends, terms), grid=...  110 us
    pallas_call x1, Pallas kernels, near_field(): pl.pallas_call(functools.partial(near_kernel, per_step, neighbours), grid...  18.8 us
    pallas_call x1, Pallas kernels, exchange(): pl.pallas_call(functools.partial(exchange_kernel, bits, tb, kc), out_shap...  16.3 us
    all_to_all x1, starting transfers between devices, body(): lax.all_to_all(payload, ('gx', 'gy', 'gz'), split_axis=0, concat_axis=0,...  7.95 us
    all_to_all x1, waiting for transfers between devices, body(): lax.all_to_all(payload, ('gx', 'gy', 'gz'), split_axis=0, concat_axis=0,...  6.19 us
    pallas_call x1, Pallas kernels, pick(): pl.pallas_call(pick_kernel, out_shape=(jax.ShapeDtypeStruct((sections, wi...  5.94 us
  transfers between devices with their start and end apart: 1, of which 1 were waited for; matrix products, arithmetic and copies ran while one was open for 0% of the time, Pallas kernels for 11%

profile of v4, /device:TPU:1, one launch (start us, length us, event | category | flops | bytes accessed | tf_op | source)
XLA Modules:
  0.0 169.4 jit_solution(4569650004459311)
XLA Ops:
  0.6 5.9 %pick.1 = (bf16[7,576,128]{2,1,0:T(8,128)(2,1)}, f32[2048,128]{1,0:T(8,128)}) custom-call(s32[7,1,384]{2,1,0:T(1,128)} %bitcast.24, s32[7,1,16]{2,1,0:T(1,128)} %bitcast.27, bf16[165,1024]{1,0:T(8,128)(2,1)} %bitcast.21, bf16[3,128,128]{2,1,0:T(8,128)(2,1)} %bitcast.17, bf16[128,128]{1,0:T(8,128)(2,1)} %bitcast.22), custom_call_target="tpu_custom_call" | custom-call | tf_op jit(solution)/shard_map/pick/pallas_call | solution.py:74
  6.6 16.3 %exchange.1 = (bf16[7,576,128]{2,1,0:T(8,128)(2,1)}, s32[16,128]{1,0:T(8,128)}, f32[1024,128]{1,0:T(8,128)}, s32[64,2048]{1,0:T(8,128)}) custom-call(bf16[7,576,128]{2,1,0:T(8,128)(2,1)} %get-tuple-element.10.send, s32[1,1024]{1,0:T(1,128)} %bitcast.25, s32[1,1024]{1,0:T(1,128)} %bitcast.26, s32[1024,128]{1,0:T(8,128)} %bitcast.20), custom_call_target="tpu_custom_call" | custom-call | tf_op jit(solution)/shard_map/exchange/pallas_call | solution.py:168
  22.9 110.0 %m2l.1 = f32[128,24,128]{2,1,0:T(8,128)} custom-call(s32[64,2048]{1,0:T(8,128)} %get-tuple-element.11.idx_hbm, s32[16,128]{1,0:T(8,128)} %get-tuple-element.12.fill, f32[2048,128]{1,0:T(8,128)} %get-tuple-element.13.own_hbm, bf16[7,576,128]{2,1,0:T(8,128)(2,1)} %get-tuple-element.14.recv.got, bf16[165,21120]{1,0:T(8,128)(2,1)} %ops_hbm.1, ...), custom_call_target="tpu_custom_call" | custom-call | tf_op jit(solution)/shard_map/m2l/pallas_call | solution.py:324
  132.9 8.0 %all-to-all-start = ((f32[128,24,128]{2,1,0:T(8,128)}), f32[128,24,128]{2,1,0:T(8,128)S(1)}, u32[]{:S(2)}, u32[]{:S(2)}) async-start(f32[128,24,128]{2,1,0:T(8,128)} %m2l.1), calls=%async_computation | async-start | bytes 3145728 | tf_op jit(solution)/shard_map/all_to_all | solution.py:561
  140.9 0.0 copy-start
  140.9 18.8 %near.1 = f32[128,128]{1,0:T(8,128)} custom-call(s32[8,128]{1,0:T(8,128)} %bitcast.30, bf16[3,128,128]{2,1,0:T(8,128)(2,1)} %bitcast.18, bf16[128,128]{1,0:T(8,128)(2,1)} %bitcast.23, bf16[7,576,128]{2,1,0:T(8,128)(2,1)} %get-tuple-element.14.recv.got), custom_call_target="tpu_custom_call" | custom-call | flops 268435456 | bytes 1048576 | tf_op jit(solution)/shard_map/near/pallas_call | solution.py:448
  159.7 6.2 %all-to-all-done.arrived = f32[128,24,128]{2,1,0:T(8,128)S(1)} async-done(((f32[128,24,128]{2,1,0:T(8,128)}), f32[128,24,128]{2,1,0:T(8,128)S(1)}, u32[]{:S(2)}, u32[]{:S(2)}) %all-to-all-start) | async-done | bytes 1572896 | tf_op jit(solution)/shard_map/all_to_all | solution.py:561
  165.9 0.0 copy-done
  165.9 0.0 copy-start.1
  165.9 0.8 copy-done.1
  166.7 2.7 %finish.1 = (f32[165,1,128]{2,1,0:T(1,128)}, f32[128,128]{1,0:T(8,128)}) custom-call(f32[128,24,128]{2,1,0:T(8,128)S(1)} %all-to-all-done.arrived, bf16[3,128,128]{2,1,0:T(8,128)(2,1)S(1)} %bitcast.19, f32[128,128]{1,0:T(8,128)S(1)} %copy-done.1), custom_call_target="tpu_custom_call" | custom-call | tf_op jit(solution)/shard_map/finish/pallas_call | solution.py:526
Async XLA Ops:
  132.9 33.0 %all-to-all-start = ((f32[128,24,128]{2,1,0:T(8,128)}), f32[128,24,128]{2,1,0:T(8,128)S(1)}, u32[]{:S(2)}, u32[]{:S(2)}) async-start(f32[128,24,128]{2,1,0:T(8,128)} %m2l.1), calls=%async_computation | async-start | bytes 3145728 | tf_op jit(solution)/shard_map/all_to_all | solution.py:561
  140.9 25.0 %copy-start = (bf16[1,1,1,128,3,128]{5,3,4,2,1,0:T(8,128)(2,1)S(1)}, bf16[1,1,1,128,3,128]{5,3,4,2,1,0:T(8,128)(2,1)}, u32[]{:S(2)}) copy-start(bf16[1,1,1,128,3,128]{5,3,4,2,1,0:T(8,128)(2,1)} %param.11) | copy-start | bytes 294916
  165.9 0.8 copy-start.1

commit v5 on v4

--- a/solution.py
+++ b/solution.py
@@ -134,8 +134,10 @@
 
 
 def exchange_kernel(
-    bits, tb, kc, send, owner, box, lists, recv, fill, labels, idx, turned, send_sem, recv_sem
+    bits, tb, kc, send, owner, box, lists_hbm, recv, fill, labels, idx, lists, turned, send_sem, recv_sem, lists_sem
 ):
+    lists_copy = pltpu.make_async_copy(lists_hbm, lists, lists_sem)
+    lists_copy.start()
     partners = []
     for name, count in bits:
         for bit in range(count):
@@ -156,8 +158,9 @@
         )
         copy.start()
         copies.append(copy)
+    fill_slots(owner, box, fill, labels)
+    lists_copy.wait()
     order_lists(tb, kc, lists, idx, turned)
-    fill_slots(owner, box, fill, labels)
     for copy in copies:
         copy.wait()
 
@@ -173,12 +176,14 @@
             jax.ShapeDtypeStruct((8 * LANES, LANES), F32),
             jax.ShapeDtypeStruct((positions // kc, kc * total), I32),
         ),
-        in_specs=[hbm(), vmem(), vmem(), vmem()],
+        in_specs=[hbm(), vmem(), vmem(), hbm()],
         out_specs=(hbm(), vmem(), vmem(), vmem()),
         scratch_shapes=[
+            pltpu.VMEM(lists.shape, I32),
             pltpu.VMEM((positions, LANES), F32),
             pltpu.SemaphoreType.DMA((sections,)),
             pltpu.SemaphoreType.DMA((sections,)),
+            pltpu.SemaphoreType.DMA,
         ],
         compiler_params=params(collective_id=0, has_side_effects=True),
         name="exchange",
@@ -459,7 +464,7 @@
         scratch_shapes=[pltpu.VMEM((count * 4, LANES), F32), pltpu.VMEM((count * FEATURES, LANES), F32)]
         + [pltpu.VMEM((neighbours * FEATURES, LANES), F32)] * at_once
         + [pltpu.VMEM((neighbours * FEATURES, neighbours * LANES), BF16)] * at_once,
-        compiler_params=params(),
+        compiler_params=pltpu.CompilerParams(vmem_limit_bytes=24 * 2**20),
         cost_estimate=pl.CostEstimate(flops=2**28, bytes_accessed=2**20, transcendentals=2**24),
         name="near",
     )(lists, coords, masses, recv)

time: 170 us -> 169 us (level)
  Pallas kernels: 154 us -> 152 us
  transfers between devices with their start and end apart: 1 -> 1, of which waited for: 1 -> 1; matrix products, arithmetic and copies ran while one was open for 0% -> 0% of each run, Pallas kernels for 11% -> 10%
where the time goes in v5:
time: 169 us; the launch traced here: 168 us
  Pallas kernels  152 us (90%)
  starting transfers between devices  8.02 us (5%)
  waiting for transfers between devices  7.35 us (4%)
    pallas_call x1, Pallas kernels, m2l(): pl.pallas_call(functools.partial(m2l_kernel, tb, kc, sends, terms), grid=...  110 us
    pallas_call x1, Pallas kernels, near_field(): pl.pallas_call(functools.partial(near_kernel, per_step, neighbours), grid...  17.6 us
    pallas_call x1, Pallas kernels, exchange(): pl.pallas_call(functools.partial(exchange_kernel, bits, tb, kc), out_shap...  16 us
    all_to_all x1, starting transfers between devices, body(): lax.all_to_all(payload, ('gx', 'gy', 'gz'), split_axis=0, concat_axis=0,...  8.02 us
    all_to_all x1, waiting for transfers between devices, body(): lax.all_to_all(payload, ('gx', 'gy', 'gz'), split_axis=0, concat_axis=0,...  7.35 us
    pallas_call x1, Pallas kernels, pick(): pl.pallas_call(pick_kernel, out_shape=(jax.ShapeDtypeStruct((sections, wi...  5.94 us
  transfers between devices with their start and end apart: 1, of which 1 were waited for; matrix products, arithmetic and copies ran while one was open for 0% of the time, Pallas kernels for 10%

profile of v5, /device:TPU:1, one launch (start us, length us, event | category | flops | bytes accessed | tf_op | source)
XLA Modules:
  0.0 168.3 jit_solution(7938815450295100975)
XLA Ops:
  0.6 5.9 %pick.1 = (bf16[7,576,128]{2,1,0:T(8,128)(2,1)}, f32[2048,128]{1,0:T(8,128)}) custom-call(s32[7,1,384]{2,1,0:T(1,128)} %bitcast.25, s32[7,1,16]{2,1,0:T(1,128)} %bitcast.28, bf16[165,1024]{1,0:T(8,128)(2,1)} %bitcast.24, bf16[3,128,128]{2,1,0:T(8,128)(2,1)} %bitcast.17, bf16[128,128]{1,0:T(8,128)(2,1)} %bitcast.20), custom_call_target="tpu_custom_call" | custom-call | tf_op jit(solution)/shard_map/pick/pallas_call | solution.py:74
  6.6 16.0 %exchange.1 = (bf16[7,576,128]{2,1,0:T(8,128)(2,1)}, s32[16,128]{1,0:T(8,128)}, f32[1024,128]{1,0:T(8,128)}, s32[64,2048]{1,0:T(8,128)}) custom-call(bf16[7,576,128]{2,1,0:T(8,128)(2,1)} %get-tuple-element.10.send, s32[1,1024]{1,0:T(1,128)} %bitcast.26, s32[1,1024]{1,0:T(1,128)} %bitcast.27, s32[1024,128]{1,0:T(8,128)} %bitcast.23), custom_call_target="tpu_custom_call" | custom-call | tf_op jit(solution)/shard_map/exchange/pallas_call | solution.py:171
  22.5 110.0 %m2l.1 = f32[128,24,128]{2,1,0:T(8,128)} custom-call(s32[64,2048]{1,0:T(8,128)} %get-tuple-element.11.idx_hbm, s32[16,128]{1,0:T(8,128)} %get-tuple-element.12.fill, f32[2048,128]{1,0:T(8,128)} %get-tuple-element.13.own_hbm, bf16[7,576,128]{2,1,0:T(8,128)(2,1)} %get-tuple-element.14.recv.got, bf16[165,21120]{1,0:T(8,128)(2,1)} %ops_hbm.1, ...), custom_call_target="tpu_custom_call" | custom-call | tf_op jit(solution)/shard_map/m2l/pallas_call | solution.py:329
  132.5 0.0 copy-start
  132.6 0.0 copy-start.1
  132.6 0.0 copy-start.2
  132.6 0.0 copy-start.3
  132.6 8.0 %all-to-all-start = ((f32[128,24,128]{2,1,0:T(8,128)}), f32[128,24,128]{2,1,0:T(8,128)S(1)}, u32[]{:S(2)}, u32[]{:S(2)}) async-start(f32[128,24,128]{2,1,0:T(8,128)} %m2l.1), calls=%async_computation | async-start | bytes 3145728 | tf_op jit(solution)/shard_map/all_to_all | solution.py:566
  140.6 0.0 copy-done
  140.6 0.0 copy-done.1
  140.6 0.0 copy-done.2
  140.6 0.0 copy-done.3
  140.7 17.6 %near.1 = f32[128,128]{1,0:T(8,128)S(1)} custom-call(s32[8,128]{1,0:T(8,128)S(1)} %bitcast.22, bf16[3,128,128]{2,1,0:T(8,128)(2,1)S(1)} %bitcast.18, bf16[128,128]{1,0:T(8,128)(2,1)S(1)} %bitcast.21, bf16[7,576,128]{2,1,0:T(8,128)(2,1)S(1)} %copy-done), custom_call_target="tpu_custom_call" | custom-call | flops 268435456 | bytes 1048576 | tf_op jit(solution)/shard_map/near/pallas_call | solution.py:453
  158.3 7.3 %all-to-all-done.arrived = f32[128,24,128]{2,1,0:T(8,128)S(1)} async-done(((f32[128,24,128]{2,1,0:T(8,128)}), f32[128,24,128]{2,1,0:T(8,128)S(1)}, u32[]{:S(2)}, u32[]{:S(2)}) %all-to-all-start) | async-done | bytes 1572896 | tf_op jit(solution)/shard_map/all_to_all | solution.py:566
  165.6 2.7 %finish.1 = (f32[165,1,128]{2,1,0:T(1,128)}, f32[128,128]{1,0:T(8,128)}) custom-call(f32[128,24,128]{2,1,0:T(8,128)S(1)} %all-to-all-done.arrived, bf16[3,128,128]{2,1,0:T(8,128)(2,1)S(1)} %bitcast.19, f32[128,128]{1,0:T(8,128)S(1)} %near.1), custom_call_target="tpu_custom_call" | custom-call | tf_op jit(solution)/shard_map/finish/pallas_call | solution.py:531
Async XLA Ops:
  132.5 8.1 %copy-start = (bf16[7,576,128]{2,1,0:T(8,128)(2,1)S(1)}, bf16[7,576,128]{2,1,0:T(8,128)(2,1)}, u32[]{:S(2)}) copy-start(bf16[7,576,128]{2,1,0:T(8,128)(2,1)} %get-tuple-element.14.recv.got) | copy-start | bytes 3096580
  132.6 8.1 %copy-start.1 = (bf16[1,1,1,128,3,128]{5,3,4,2,1,0:T(8,128)(2,1)S(1)}, bf16[1,1,1,128,3,128]{5,3,4,2,1,0:T(8,128)(2,1)}, u32[]{:S(2)}) copy-start(bf16[1,1,1,128,3,128]{5,3,4,2,1,0:T(8,128)(2,1)} %param.11) | copy-start | bytes 294916
  132.6 8.1 %copy-start.2 = (bf16[1,1,1,128,128]{4,3,2,1,0:T(8,128)(2,1)S(1)}, bf16[1,1,1,128,128]{4,3,2,1,0:T(8,128)(2,1)}, u32[]{:S(2)}) copy-start(bf16[1,1,1,128,128]{4,3,2,1,0:T(8,128)(2,1)} %param.12) | copy-start | bytes 98308
  132.6 8.1 %copy-start.3 = (s32[1,1,1,128,8]{3,4,2,1,0:T(8,128)S(1)}, s32[1,1,1,128,8]{3,4,2,1,0:T(8,128)}, u32[]{:S(2)}) copy-start(s32[1,1,1,128,8]{3,4,2,1,0:T(8,128)} %param.17) | copy-start | bytes 12292
  132.6 33.0 %all-to-all-start = ((f32[128,24,128]{2,1,0:T(8,128)}), f32[128,24,128]{2,1,0:T(8,128)S(1)}, u32[]{:S(2)}, u32[]{:S(2)}) async-start(f32[128,24,128]{2,1,0:T(8,128)} %m2l.1), calls=%async_computation | async-start | bytes 3145728 | tf_op jit(solution)/shard_map/all_to_all | solution.py:566

commit v6 on v5

--- a/solution.py
+++ b/solution.py
@@ -33,9 +33,12 @@
     return pl.BlockSpec(memory_space=pl.ANY)
 
 
-def pick_kernel(cell_idx, leaf_idx, terms, coords, masses, out, pool, stage, leaves, leaf_stage):
+def pick_kernel(cells_hbm, leaf_idx, terms, coords, masses, out, pool, stage, leaves, leaf_stage, sem, *cell_idx):
     count = terms.shape[1]
-    sections, _, sends = cell_idx.shape
+    sections, _, sends = cells_hbm.shape
+    copies = [pltpu.make_async_copy(cells_hbm.at[b, 0], cell_idx[b], sem.at[b]) for b in range(sections)]
+    for copy in copies:
+        copy.start()
     psends = leaf_idx.shape[2]
     boxes = masses.shape[0]
     for r in range(0, count, 256):
@@ -50,10 +53,10 @@
 
     third = sends // 3
 
-    @pl.loop(0, sections)
-    def _(b):
+    for b in range(sections):
+        copies[b].wait()
         for r in range(sends):
-            c = cell_idx[b, 0, r] * 2
+            c = cell_idx[b][r] * 2
             stage[2 * r : 2 * r + 2, :] = pool[pl.ds(pl.multiple_of(c, 2), 2), :]
         for u in range(psends):
             c = leaf_idx[b, 0, u] * 4
@@ -77,13 +80,15 @@
             jax.ShapeDtypeStruct((sections, width, LANES), BF16),
             jax.ShapeDtypeStruct((2 * terms.shape[1], LANES), F32),
         ),
-        in_specs=[smem(), smem(), vmem(), vmem(), vmem()],
+        in_specs=[hbm(), smem(), vmem(), vmem(), vmem()],
         out_specs=(vmem(), vmem()),
         scratch_shapes=[
             pltpu.VMEM((2 * sends, LANES), F32),
             pltpu.VMEM((4 * boxes, LANES), F32),
             pltpu.VMEM((4 * psends, LANES), F32),
-        ],
+            pltpu.SemaphoreType.DMA((sections,)),
+        ]
+        + [pltpu.SMEM((sends,), I32)] * sections,
         compiler_params=params(),
         name="pick",
     )(cell_idx, leaf_idx, terms, coords, masses)

time: 169 us -> 169 us (level)
  no operation moved by 1% of the time
where the time goes in v6:
time: 169 us; the launch traced here: 168 us
  Pallas kernels  152 us (90%)
  starting transfers between devices  8.05 us (5%)
  waiting for transfers between devices  7.37 us (4%)
    pallas_call x1, Pallas kernels, m2l(): pl.pallas_call(functools.partial(m2l_kernel, tb, kc, sends, terms), grid=...  110 us
    pallas_call x1, Pallas kernels, near_field(): pl.pallas_call(functools.partial(near_kernel, per_step, neighbours), grid...  17.6 us
    pallas_call x1, Pallas kernels, exchange(): pl.pallas_call(functools.partial(exchange_kernel, bits, tb, kc), out_shap...  16 us
    all_to_all x1, starting transfers between devices, body(): lax.all_to_all(payload, ('gx', 'gy', 'gz'), split_axis=0, concat_axis=0,...  8.05 us
    all_to_all x1, waiting for transfers between devices, body(): lax.all_to_all(payload, ('gx', 'gy', 'gz'), split_axis=0, concat_axis=0,...  7.37 us
    pallas_call x1, Pallas kernels, pick(): pl.pallas_call(pick_kernel, out_shape=(jax.ShapeDtypeStruct((sections, wi...  6.08 us
  transfers between devices with their start and end apart: 1, of which 1 were waited for; matrix products, arithmetic and copies ran while one was open for 0% of the time, Pallas kernels for 10%

profile of v6, /device:TPU:1, one launch (start us, length us, event | category | flops | bytes accessed | tf_op | source)
XLA Modules:
  0.0 168.5 jit_solution(11455830664028037513)
XLA Ops:
  0.6 6.1 %pick.1 = (bf16[7,576,128]{2,1,0:T(8,128)(2,1)}, f32[2048,128]{1,0:T(8,128)}) custom-call(s32[7,1,384]{2,1,0:T(1,128)} %bitcast.25, s32[7,1,16]{2,1,0:T(1,128)} %bitcast.28, bf16[165,1024]{1,0:T(8,128)(2,1)} %bitcast.24, bf16[3,128,128]{2,1,0:T(8,128)(2,1)} %bitcast.17, bf16[128,128]{1,0:T(8,128)(2,1)} %bitcast.20), custom_call_target="tpu_custom_call" | custom-call | tf_op jit(solution)/shard_map/pick/pallas_call | solution.py:77
  6.7 16.0 %exchange.1 = (bf16[7,576,128]{2,1,0:T(8,128)(2,1)}, s32[16,128]{1,0:T(8,128)}, f32[1024,128]{1,0:T(8,128)}, s32[64,2048]{1,0:T(8,128)}) custom-call(bf16[7,576,128]{2,1,0:T(8,128)(2,1)} %get-tuple-element.10.send, s32[1,1024]{1,0:T(1,128)} %bitcast.26, s32[1,1024]{1,0:T(1,128)} %bitcast.27, s32[1024,128]{1,0:T(8,128)} %bitcast.23), custom_call_target="tpu_custom_call" | custom-call | tf_op jit(solution)/shard_map/exchange/pallas_call | solution.py:176
  22.8 109.9 %m2l.1 = f32[128,24,128]{2,1,0:T(8,128)} custom-call(s32[64,2048]{1,0:T(8,128)} %get-tuple-element.11.idx_hbm, s32[16,128]{1,0:T(8,128)} %get-tuple-element.12.fill, f32[2048,128]{1,0:T(8,128)} %get-tuple-element.13.own_hbm, bf16[7,576,128]{2,1,0:T(8,128)(2,1)} %get-tuple-element.14.recv.got, bf16[165,21120]{1,0:T(8,128)(2,1)} %ops_hbm.1, ...), custom_call_target="tpu_custom_call" | custom-call | tf_op jit(solution)/shard_map/m2l/pallas_call | solution.py:334
  132.7 0.0 copy-start
  132.7 0.0 copy-start.1
  132.7 0.0 copy-start.2
  132.7 0.0 copy-start.3
  132.7 8.0 %all-to-all-start = ((f32[128,24,128]{2,1,0:T(8,128)}), f32[128,24,128]{2,1,0:T(8,128)S(1)}, u32[]{:S(2)}, u32[]{:S(2)}) async-start(f32[128,24,128]{2,1,0:T(8,128)} %m2l.1), calls=%async_computation | async-start | bytes 3145728 | tf_op jit(solution)/shard_map/all_to_all | solution.py:571
  140.8 0.0 copy-done
  140.8 0.0 copy-done.1
  140.8 0.0 copy-done.2
  140.8 0.0 copy-done.3
  140.8 17.6 %near.1 = f32[128,128]{1,0:T(8,128)S(1)} custom-call(s32[8,128]{1,0:T(8,128)S(1)} %bitcast.22, bf16[3,128,128]{2,1,0:T(8,128)(2,1)S(1)} %bitcast.18, bf16[128,128]{1,0:T(8,128)(2,1)S(1)} %bitcast.21, bf16[7,576,128]{2,1,0:T(8,128)(2,1)S(1)} %copy-done), custom_call_target="tpu_custom_call" | custom-call | flops 268435456 | bytes 1048576 | tf_op jit(solution)/shard_map/near/pallas_call | solution.py:458
  158.4 7.4 %all-to-all-done.arrived = f32[128,24,128]{2,1,0:T(8,128)S(1)} async-done(((f32[128,24,128]{2,1,0:T(8,128)}), f32[128,24,128]{2,1,0:T(8,128)S(1)}, u32[]{:S(2)}, u32[]{:S(2)}) %all-to-all-start) | async-done | bytes 1572896 | tf_op jit(solution)/shard_map/all_to_all | solution.py:571
  165.8 2.7 %finish.1 = (f32[165,1,128]{2,1,0:T(1,128)}, f32[128,128]{1,0:T(8,128)}) custom-call(f32[128,24,128]{2,1,0:T(8,128)S(1)} %all-to-all-done.arrived, bf16[3,128,128]{2,1,0:T(8,128)(2,1)S(1)} %bitcast.19, f32[128,128]{1,0:T(8,128)S(1)} %near.1), custom_call_target="tpu_custom_call" | custom-call | tf_op jit(solution)/shard_map/finish/pallas_call | solution.py:536
Async XLA Ops:
  132.7 8.1 %copy-start = (bf16[7,576,128]{2,1,0:T(8,128)(2,1)S(1)}, bf16[7,576,128]{2,1,0:T(8,128)(2,1)}, u32[]{:S(2)}) copy-start(bf16[7,576,128]{2,1,0:T(8,128)(2,1)} %get-tuple-element.14.recv.got) | copy-start | bytes 3096580
  132.7 8.1 %copy-start.1 = (bf16[1,1,1,128,3,128]{5,3,4,2,1,0:T(8,128)(2,1)S(1)}, bf16[1,1,1,128,3,128]{5,3,4,2,1,0:T(8,128)(2,1)}, u32[]{:S(2)}) copy-start(bf16[1,1,1,128,3,128]{5,3,4,2,1,0:T(8,128)(2,1)} %param.11) | copy-start | bytes 294916
  132.7 8.1 %copy-start.2 = (bf16[1,1,1,128,128]{4,3,2,1,0:T(8,128)(2,1)S(1)}, bf16[1,1,1,128,128]{4,3,2,1,0:T(8,128)(2,1)}, u32[]{:S(2)}) copy-start(bf16[1,1,1,128,128]{4,3,2,1,0:T(8,128)(2,1)} %param.12) | copy-start | bytes 98308
  132.7 8.1 %copy-start.3 = (s32[1,1,1,128,8]{3,4,2,1,0:T(8,128)S(1)}, s32[1,1,1,128,8]{3,4,2,1,0:T(8,128)}, u32[]{:S(2)}) copy-start(s32[1,1,1,128,8]{3,4,2,1,0:T(8,128)} %param.17) | copy-start | bytes 12292
  132.7 33.0 %all-to-all-start = ((f32[128,24,128]{2,1,0:T(8,128)}), f32[128,24,128]{2,1,0:T(8,128)S(1)}, u32[]{:S(2)}, u32[]{:S(2)}) async-start(f32[128,24,128]{2,1,0:T(8,128)} %m2l.1), calls=%async_computation | async-start | bytes 3145728 | tf_op jit(solution)/shard_map/all_to_all | solution.py:571
